TPU v7x, 128 devices: a whole 4x4x4 slice. The times are simulated.
128 devices in a mesh: row: 8 (over x, y_lo), col: 16 (over y_hi, z, core).
Axes of the slice: x: 4, y: 4 (y_hi: 2, y_lo: 2; y = y_hi * 2 + y_lo), z: 4, core: 2. Of those that a mesh axis runs over, the one named last changes fastest.
Arguments:
- record: bfloat16 [180224, 4096], P(('row', 'col')), may hold values from -6 to 6
- fir_taps: float32 [101], replicated, may hold values from -0.625 to 0.625
- bins: int32 [16], replicated, may hold values from 1 to 639
- offsets: int32 [128], P(('row', 'col')), may hold values from 0 to 28, as said below
Outputs:
- cross: bfloat16 [16, 2, 4096, 4096], P(None, None, 'row', 'col')
Inputs may be any that keep to these rules, and one draw needn't show every extreme that they name: `offsets`: a window's start offset within its slot of 1408 samples.
All inputs are finite; a program needn't handle non-finite values.
Results may differ from a plain program's by a relative error of at most 0.0069.
Values may be sent and summed in bfloat16 or wider, within the bound.
A program may use at most 192 MiB of HBM per device.

v0:
```python
import math

import jax
import jax.numpy as jnp
from jax import lax
from jax.sharding import PartitionSpec as P

F = 16
WL = 1280
TAPS = 101


floor_level = 0.5


def analysis_kernel(fir_taps, bins):
    span = WL + TAPS - 1
    sample_times = jnp.arange(WL, dtype=jnp.int32)
    phase_index = bins[:, None] * sample_times[None, :] % WL
    angles = 2.0 * math.pi / WL * phase_index.astype(jnp.float32)
    centre = (jnp.arange(WL, dtype=jnp.float32) + 0.5) / WL
    window_taper = (0.5 - 0.5 * jnp.cos(2.0 * math.pi * centre)) / math.sqrt(WL)
    pattern = jnp.stack([jnp.cos(angles) * window_taper, -jnp.sin(angles) * window_taper]).reshape(
        2 * F, WL
    )
    lanes = 128
    blocks = pl_cdiv(span, lanes)
    width = 2 * lanes
    padded = jnp.pad(pattern, ((0, 0), (TAPS - 1, blocks * lanes + lanes - WL - (TAPS - 1))))
    windows = jnp.concatenate(
        [
            padded[:, : blocks * lanes].reshape(2 * F, blocks, lanes),
            padded[:, lanes : (blocks + 1) * lanes].reshape(2 * F, blocks, lanes),
        ],
        axis=2,
    )
    vector = jnp.concatenate([fir_taps, jnp.zeros((width + 1 - TAPS,), jnp.float32)])
    band = jnp.tile(vector, lanes)[: lanes * width].reshape(lanes, width)
    kernel = jnp.einsum(
        "bqs,rs->bqr",
        windows,
        band,
        precision=lax.Precision.HIGHEST,
        preferred_element_type=jnp.float32,
    ).reshape(2 * F, blocks * lanes)[:, :span]
    return kernel.astype(jnp.bfloat16)


def pl_cdiv(a, b):
    return (a + b - 1) // b


def whiten(spectra):
    shaped = spectra.reshape(spectra.shape[0], 2, F, spectra.shape[-1])
    magnitude = jnp.sqrt(shaped[:, 0] * shaped[:, 0] + shaped[:, 1] * shaped[:, 1])
    inverse = 1.0 / jnp.maximum(magnitude, floor_level)
    return (shaped * inverse[:, None]).astype(jnp.bfloat16)


def on_device(record, fir_taps, bins, offsets):
    kernel = analysis_kernel(fir_taps, bins)
    span = WL + TAPS - 1
    local_count = offsets.shape[0]

    def one_window(window):
        first_row = window * WL + offsets[window]
        samples = lax.dynamic_slice_in_dim(record, first_row, span, 0)
        return jnp.dot(kernel, samples, preferred_element_type=jnp.float32)

    spectra = lax.map(one_window, jnp.arange(local_count, dtype=jnp.int32))
    whitened = whiten(spectra)
    channels = whitened.shape[-1]
    row_count = lax.axis_size("row")
    col_count = lax.axis_size("col")
    total_windows = local_count * row_count * col_count
    row_part = lax.all_to_all(
        whitened.reshape(local_count, 2, F, row_count, channels // row_count),
        "row", split_axis=3, concat_axis=0, tiled=True,
    )
    row_block = lax.all_gather(row_part, "col", axis=0, tiled=False)
    col_part = lax.all_to_all(
        whitened.reshape(local_count, 2, F, col_count, channels // col_count),
        "col", split_axis=3, concat_axis=0, tiled=True,
    )
    col_block = lax.all_gather(col_part, "row", axis=0, tiled=False)
    left = row_block.reshape(col_count, row_count, local_count, 2, F, channels // row_count)
    right = col_block.reshape(row_count, col_count, local_count, 2, F, channels // col_count)
    right2 = jnp.stack(
        [right, jnp.stack([right[:, :, :, 1], -right[:, :, :, 0]], axis=3)], axis=5
    )
    cross_sum = jnp.einsum(
        "crwkfi,rcwkfpj->fpij", left, right2, preferred_element_type=jnp.float32
    )
    return (cross_sum * (1.0 / total_windows)).astype(jnp.bfloat16)


def solution(mesh):
    placed = (P(("row", "col"), None), P(), P(), P(("row", "col")))
    return jax.shard_map(
        on_device,
        mesh=mesh,
        in_specs=placed,
        out_specs=P(None, None, "row", "col"),
        check_vma=False,
    )
```

profile of v0, /device:TPU:0, one launch (start us, length us, event | category | flops | bytes accessed | tf_op | source)
XLA Modules:
  0.0 175.1 jit_solution(11061920724869796084)
XLA Ops:
  6.5 0.0 all-gather.5.cloned.1.call-start
  6.5 0.1 subtract_multiply_fusion
  7.2 0.7 concatenate.7
  7.9 0.3 tile.10
  8.3 1.1 cosine_multiply_fusion
  9.4 0.1 fusion.17
  9.6 0.5 fusion.7
  10.1 7.4 %fusion.1 = f32[32,4096]{1,0:T(8,128)S(1)} fusion(bf16[1408,4096]{1,0:T(8,128)(2,1)} %param.4, s32[]{:T(128)S(6)} %select_n.25, bf16[32,1408]{1,0:T(8,128)(2,1)S(1)} %bitcast.78), kind=kOutput, calls=%fused_computation.2 | convolution fusion | flops 361758720 | bytes 11952132 | tf_op jit(solution)/shard_map/while/body/eval_jaxpr/dot_general | solution.py:68
  17.6 0.1 fusion.16
  17.7 0.1 copy.50
  17.8 0.2 copy.32
  17.9 0.2 copy.49
  18.1 0.3 fusion.9
  18.4 17.6 %all_to_all.30 = bf16[1,2,16,16,256]{4,2,1,0,3:T(8,128)(2,1)} all-to-all(bf16[1,2,16,16,256]{4,2,1,0,3:T(8,128)(2,1)S(1)} %fusion.9), channel_id=1, replica_groups=mesh['row'=8,'col'=16] {'col'}, dimensions={3} | all-to-all | bytes 524288 | tf_op jit(solution)/shard_map/all_to_all | solution.py:81
  36.0 0.0 all-gather.5.cloned.1.call-update
  36.1 0.0 all-gather.7.cloned.1.call-start
  36.1 0.2 copy.52
  36.3 0.2 copy.37
  36.4 0.3 copy.51
  36.8 0.3 fusion.8
  37.1 13.8 %all_to_all.31 = bf16[1,2,16,8,512]{4,2,1,0,3:T(8,128)(2,1)} all-to-all(bf16[1,2,16,8,512]{4,2,1,0,3:T(8,128)(2,1)S(1)} %fusion.8), channel_id=1, replica_groups=mesh['row'=8,'col'=16] {'row'}, dimensions={3} | all-to-all | bytes 524288 | tf_op jit(solution)/shard_map/all_to_all | solution.py:76
  50.9 0.0 all-gather.7.cloned.1.call-update
  50.9 35.3 %all-gather.5.cloned.1.call-done = bf16[128,1,2,16,1,256]{5,3,4,2,1,0:T(8,128)(2,1)} async-done(((bf16[16,1,2,16,1,256]{5,3,4,2,1,0:T(8,128)(2,1)}), bf16[128,1,2,16,1,256]{5,3,4,2,1,0:T(8,128)(2,1)}) %all-gather.5.cloned.1.call-update) | async-done | bytes 2097168 | tf_op jit(solution)/shard_map/all_gather | solution.py:85
  86.3 2.8 %copy.35 = bf16[128,1,2,16,1,256]{5,0,2,3,4,1:T(8,128)(2,1)S(1)} copy(bf16[128,1,2,16,1,256]{5,3,4,2,1,0:T(8,128)(2,1)} %all-gather.5.cloned.1.call-done) | data formatting | bytes 4194304 | tf_op jit(solution)/shard_map/all_gather | solution.py:85
  89.0 0.1 fusion.28
  89.2 1.5 maximum_bitcast_fusion.2
  90.7 52.9 %all-gather.7.cloned.1.call-done = bf16[128,1,2,16,1,512]{5,3,4,2,1,0:T(8,128)(2,1)} async-done(((bf16[8,1,2,16,1,512]{5,3,4,2,1,0:T(8,128)(2,1)}), bf16[128,1,2,16,1,512]{5,3,4,2,1,0:T(8,128)(2,1)}) %all-gather.7.cloned.1.call-update) | async-done | bytes 4194320 | tf_op jit(solution)/shard_map/all_gather | solution.py:80
  143.6 12.4 %fusion.3 = bf16[16,2,512,256]{2,3,1,0:T(8,128)(2,1)} fusion(bf16[8,16,1,2,16,1,256]{6,1,0,3,5,4,2:T(8,128)(2,1)} %maximum_bitcast_fusion.2, bf16[8,16,1,2,16,1,256]{6,1,0,3,5,4,2:T(8,128)(2,1)S(1)} %bitcast.65, bf16[16,8,2,16,512,1]{4,3,2,1,0,5:T(8,128)(2,1)} %bitcast.79), kind=kOutput, calls=%fused_computation.4 | convolution fusion | flops 2157969408 | bytes 16777216 | tf_op jit(solution)/shard_map/crwkfi,rcwkfpj->fpij/dot_general | solution.py:91
  156.0 12.2 %copy.41 = bf16[16,2,512,256]{3,2,1,0:T(8,128)(2,1)} copy(bf16[16,2,512,256]{2,3,1,0:T(8,128)(2,1)} %fusion.3) | data formatting | bytes 16777216 | tf_op jit(solution)/shard_map/convert_element_type | solution.py:94
  (6 shorter events, 0.1 us)
Async XLA Ops:
  6.5 79.7 %all-gather.5.cloned.1.call-start = ((), (), s32[]{:S(2)}) async-start(), calls=%async_computation.2 | async-start | bytes 2359296 | tf_op jit(solution)/shard_map/all_gather | solution.py:85
  36.1 107.5 %all-gather.7.cloned.1.call-start = ((), (), s32[]{:S(2)}) async-start(), calls=%async_computation.3 | async-start | bytes 4456448 | tf_op jit(solution)/shard_map/all_gather | solution.py:80
Sparse Core Ops, SparseCore 0:
  36.2 50.0 all-gather.4
  88.7 54.7 all-gather.6
where the time goes:
time: 177 us; the launch traced here: 175 us
  waiting for transfers between devices  88.2 us (50%)
  blocking collectives  31.4 us (18%)
  matrix products  20.3 us (11%)
  local copies, waits for them, and re-layouts  17.3 us (10%)
  between operations  14.2 us (8%)
  other arithmetic  3.53 us (2%)
    all_gather x1, waiting for transfers between devices, on_device(): row_block = lax.all_gather(row_part, 'col', axis=0, tiled=False)  52.9 us
    all_gather x1, waiting for transfers between devices, on_device(): col_block = lax.all_gather(col_part, 'row', axis=0, tiled=False)  35.3 us
    all_to_all x1, blocking collectives, on_device(): lax.all_to_all(whitened.reshape(local_count, 2, F, col_count, channels //...  17.6 us
    all_to_all x1, blocking collectives, on_device(): lax.all_to_all(whitened.reshape(local_count, 2, F, row_count, channels //...  13.8 us
    dot_general x1, matrix products, on_device(): jnp.einsum('crwkfi,rcwkfpj->fpij', left, right2, preferred_element_type=j...  12.4 us
    convert_element_type x1, local copies, waits for them, and re-layouts, on_device(): return (cross_sum * (1.0 / total_windows)).astype(jnp.bfloat16)  12.2 us
    dot_general x1, matrix products, one_window(): return jnp.dot(kernel, samples, preferred_element_type=jnp.float32)  7.44 us
  transfers between devices with their start and end apart: 2, of which 2 were waited for; matrix products, arithmetic and copies ran while one was open for 3% of the time, Pallas kernels for 0%

commit v1 on v0

--- a/solution.py
+++ b/solution.py
@@ -1,9 +1,12 @@
+import functools
 import math
 
 import jax
 import jax.numpy as jnp
 from jax import lax
 from jax.sharding import PartitionSpec as P
+from jax.experimental import pallas as pl
+from jax.experimental.pallas import tpu as pltpu
 
 F = 16
 WL = 1280
@@ -57,6 +60,90 @@
     return (shaped * inverse[:, None]).astype(jnp.bfloat16)
 
 
+MESH = pl.DeviceIdType.MESH
+
+
+def exchange_kernel(nr, nc, w_ref, rbuf, cbuf, r1, c1, r2, c2, s1r, s1c, s2r, s2c, loc):
+    r = lax.axis_index("row")
+    c = lax.axis_index("col")
+    rb = rbuf.shape[-1]
+    cb = cbuf.shape[-1]
+    own_r = pltpu.make_async_copy(w_ref.at[:, pl.ds(r * rb, rb)], rbuf.at[c, r], loc.at[0])
+    own_r.start()
+    own_c = pltpu.make_async_copy(w_ref.at[:, pl.ds(c * cb, cb)], cbuf.at[r, c], loc.at[1])
+    own_c.start()
+    sends = []
+    for d in range(1, nr):
+        t = lax.rem(r + d, nr)
+        cp = pltpu.make_async_remote_copy(
+            src_ref=w_ref.at[:, pl.ds(t * rb, rb)], dst_ref=rbuf.at[c, r],
+            send_sem=s1r.at[d], recv_sem=r1.at[r], device_id=(t, c), device_id_type=MESH,
+        )
+        cp.start()
+        sends.append(cp)
+    for d in range(1, nc):
+        t = lax.rem(c + d, nc)
+        cp = pltpu.make_async_remote_copy(
+            src_ref=w_ref.at[:, pl.ds(t * cb, cb)], dst_ref=cbuf.at[r, c],
+            send_sem=s1c.at[d], recv_sem=c1.at[c], device_id=(r, t), device_id_type=MESH,
+        )
+        cp.start()
+        sends.append(cp)
+    own_r.wait()
+    for d in range(1, nr):
+        src = lax.rem(r + nr - d, nr)
+        pltpu.make_async_copy(rbuf.at[c, src], rbuf.at[c, src], r1.at[src]).wait()
+    for d in range(1, nc):
+        t = lax.rem(c + d, nc)
+        cp = pltpu.make_async_remote_copy(
+            src_ref=rbuf.at[c], dst_ref=rbuf.at[c],
+            send_sem=s2r.at[d], recv_sem=r2.at[c], device_id=(r, t), device_id_type=MESH,
+        )
+        cp.start()
+        sends.append(cp)
+    own_c.wait()
+    for d in range(1, nc):
+        src = lax.rem(c + nc - d, nc)
+        pltpu.make_async_copy(cbuf.at[r, src], cbuf.at[r, src], c1.at[src]).wait()
+    for d in range(1, nr):
+        t = lax.rem(r + d, nr)
+        cp = pltpu.make_async_remote_copy(
+            src_ref=cbuf.at[r], dst_ref=cbuf.at[r],
+            send_sem=s2c.at[d], recv_sem=c2.at[r], device_id=(t, c), device_id_type=MESH,
+        )
+        cp.start()
+        sends.append(cp)
+    for cp in sends:
+        cp.wait_send()
+    for d in range(1, nc):
+        src = lax.rem(c + nc - d, nc)
+        pltpu.make_async_copy(rbuf.at[src], rbuf.at[src], r2.at[src]).wait()
+    for d in range(1, nr):
+        src = lax.rem(r + nr - d, nr)
+        pltpu.make_async_copy(cbuf.at[src], cbuf.at[src], c2.at[src]).wait()
+
+
+def exchange(w, nr, nc):
+    rows, channels = w.shape
+    rb = channels // nr
+    cb = channels // nc
+    dma = pltpu.SemaphoreType.DMA
+    return pl.pallas_call(
+        functools.partial(exchange_kernel, nr, nc),
+        out_shape=(
+            jax.ShapeDtypeStruct((nc, nr, rows, rb), w.dtype),
+            jax.ShapeDtypeStruct((nr, nc, rows, cb), w.dtype),
+        ),
+        in_specs=[pl.BlockSpec(memory_space=pl.ANY)],
+        out_specs=(pl.BlockSpec(memory_space=pl.ANY), pl.BlockSpec(memory_space=pl.ANY)),
+        scratch_shapes=[
+            dma((nr,)), dma((nc,)), dma((nc,)), dma((nr,)),
+            dma((nr,)), dma((nc,)), dma((nc,)), dma((nr,)), dma((2,)),
+        ],
+        compiler_params=pltpu.CompilerParams(has_side_effects=True),
+    )(w)
+
+
 def on_device(record, fir_taps, bins, offsets):
     kernel = analysis_kernel(fir_taps, bins)
     span = WL + TAPS - 1
@@ -73,16 +160,9 @@
     row_count = lax.axis_size("row")
     col_count = lax.axis_size("col")
     total_windows = local_count * row_count * col_count
-    row_part = lax.all_to_all(
-        whitened.reshape(local_count, 2, F, row_count, channels // row_count),
-        "row", split_axis=3, concat_axis=0, tiled=True,
+    row_block, col_block = exchange(
+        whitened.reshape(2 * F, channels), row_count, col_count
     )
-    row_block = lax.all_gather(row_part, "col", axis=0, tiled=False)
-    col_part = lax.all_to_all(
-        whitened.reshape(local_count, 2, F, col_count, channels // col_count),
-        "col", split_axis=3, concat_axis=0, tiled=True,
-    )
-    col_block = lax.all_gather(col_part, "row", axis=0, tiled=False)
     left = row_block.reshape(col_count, row_count, local_count, 2, F, channels // row_count)
     right = col_block.reshape(row_count, col_count, local_count, 2, F, channels // col_count)
     right2 = jnp.stack(

time: 177 us -> 146 us (0.82)
  the two profiles are of different devices: /device:TPU:0 before, /device:TPU:54 now
where the time goes in v1:
time: 146 us
  Pallas kernels  103 us (71%)
  matrix products  22.7 us (16%)
  local copies, waits for them, and re-layouts  17 us (12%)
  other arithmetic  2.56 us (2%)
    pallas_call x1, Pallas kernels, exchange(): pl.pallas_call(functools.partial(exchange_kernel, nr, nc), out_shape=(jax...  103 us
    dot_general x1, matrix products, on_device(): jnp.einsum('crwkfi,rcwkfpj->fpij', left, right2, preferred_element_type=j...  14.8 us
    convert_element_type x1, local copies, waits for them, and re-layouts, on_device(): return (cross_sum * (1.0 / total_windows)).astype(jnp.bfloat16)  12.2 us
    dot_general x1, matrix products, one_window(): return jnp.dot(kernel, samples, preferred_element_type=jnp.float32)  7.48 us

profile of v1, /device:TPU:54, one launch (start us, length us, event | category | flops | bytes accessed | tf_op | source)
XLA Modules:
  0.0 145.6 jit_solution(8411147634617366586)
XLA Ops:
  0.7 0.7 concatenate.7
  1.3 0.1 subtract_multiply_fusion
  1.4 1.1 cosine_multiply_fusion
  2.5 0.3 tile.10
  2.9 0.1 fusion.17
  3.1 0.5 fusion.7
  3.6 7.5 %fusion.1 = f32[32,4096]{1,0:T(8,128)S(1)} fusion(bf16[1408,4096]{1,0:T(8,128)(2,1)} %param.4, s32[]{:T(128)S(6)} %select_n.25, bf16[32,1408]{1,0:T(8,128)(2,1)S(1)} %bitcast.50), kind=kOutput, calls=%fused_computation.2 | convolution fusion | flops 361758720 | bytes 11952132 | tf_op jit(solution)/shard_map/while/body/eval_jaxpr/dot_general | solution.py:155
  11.1 0.1 fusion.16
  11.2 0.8 fusion.8.w_ref
  11.9 102.5 %shard_map.46 = (bf16[16,8,32,512]{3,2,1,0:T(8,128)(2,1)}, bf16[8,16,32,256]{3,2,1,0:T(8,128)(2,1)}) custom-call(bf16[32,4096]{1,0:T(8,128)(2,1)} %fusion.8.w_ref), custom_call_target="tpu_custom_call" | custom-call | tf_op jit(solution)/shard_map/pallas_call | solution.py:131
  114.5 0.0 copy-start
  114.5 2.9 %copy.15 = bf16[8,16,1,2,16,1,256]{6,1,0,3,5,4,2:T(8,128)(2,1)S(1)} copy(bf16[8,16,1,2,16,1,256]{6,4,3,1,0,5,2:T(8,128)(2,1)} %bitcast.46) | data formatting | bytes 4194304 | tf_op jit(solution)/shard_map/stack;reshape | solution.py:168
  117.4 0.0 copy-done
  117.4 0.2 fusion.28
  117.7 0.3 copy.22
  118.0 0.3 copy_negate_fusion
  118.3 0.2 maximum_bitcast_fusion.2
  118.6 14.8 %fusion.3 = bf16[16,2,512,256]{2,3,1,0:T(8,128)(2,1)} fusion(bf16[8,16,1,2,16,1,256]{6,1,0,3,5,4,2:T(8,128)(2,1)S(1)} %maximum_bitcast_fusion.2, bf16[8,16,1,2,16,1,256]{6,1,0,3,5,4,2:T(8,128)(2,1)S(1)} %copy.15, bf16[16,8,2,16,512,1]{4,3,2,1,0,5:T(8,128)(2,1)} %bitcast.51), kind=kOutput, calls=%fused_computation.4 | convolution fusion | flops 2157969408 | bytes 16777216 | tf_op jit(solution)/shard_map/crwkfi,rcwkfpj->fpij/dot_general | solution.py:171
  133.4 12.2 %copy.17 = bf16[16,2,512,256]{3,2,1,0:T(8,128)(2,1)} copy(bf16[16,2,512,256]{2,3,1,0:T(8,128)(2,1)} %fusion.3) | data formatting | bytes 16777216 | tf_op jit(solution)/shard_map/convert_element_type | solution.py:174
  (6 shorter events, 0.1 us)
Async XLA Ops:
  114.5 2.9 %copy-start = (bf16[8,16,32,256]{3,2,1,0:T(8,128)(2,1)S(1)}, bf16[8,16,32,256]{3,2,1,0:T(8,128)(2,1)}, u32[]{:S(2)}) copy-start(bf16[8,16,32,256]{3,2,1,0:T(8,128)(2,1)} %get-tuple-element.20) | copy-start | bytes 6291460

commit v2 on v1

--- a/solution.py
+++ b/solution.py
@@ -163,15 +163,49 @@
     row_block, col_block = exchange(
         whitened.reshape(2 * F, channels), row_count, col_count
     )
-    left = row_block.reshape(col_count, row_count, local_count, 2, F, channels // row_count)
-    right = col_block.reshape(row_count, col_count, local_count, 2, F, channels // col_count)
-    right2 = jnp.stack(
-        [right, jnp.stack([right[:, :, :, 1], -right[:, :, :, 0]], axis=3)], axis=5
-    )
-    cross_sum = jnp.einsum(
-        "crwkfi,rcwkfpj->fpij", left, right2, preferred_element_type=jnp.float32
-    )
-    return (cross_sum * (1.0 / total_windows)).astype(jnp.bfloat16)
+    windows = row_count * col_count * local_count
+    rb = channels // row_count
+    cb = channels // col_count
+    left = row_block.reshape(windows, 2 * F, rb).transpose(1, 2, 0)
+    right = (
+        col_block.reshape(row_count, col_count, 2 * F, cb)
+        .transpose(2, 1, 0, 3)
+        .reshape(2 * F, windows, cb)
+    )
+    return cross(left, right, 1.0 / total_windows)
+
+
+def cross_kernel(scale, l0, l1, r0, r1, out_ref):
+    def dot(a, b):
+        return jnp.dot(a[0], b[0], preferred_element_type=jnp.float32)
+
+    real = dot(l0, r0) + dot(l1, r1)
+    imag = dot(l0, r1) - dot(l1, r0)
+    out_ref[0, 0] = (real * scale).astype(out_ref.dtype)
+    out_ref[0, 1] = (imag * scale).astype(out_ref.dtype)
+
+
+def cross(left, right, scale):
+    parts, rb, windows = left.shape
+    cb = right.shape[-1]
+    bins = parts // 2
+    return pl.pallas_call(
+        functools.partial(cross_kernel, scale),
+        out_shape=jax.ShapeDtypeStruct((bins, 2, rb, cb), jnp.bfloat16),
+        grid=(bins,),
+        in_specs=[
+            pl.BlockSpec((1, rb, windows), lambda f: (f, 0, 0)),
+            pl.BlockSpec((1, rb, windows), lambda f: (f + bins, 0, 0)),
+            pl.BlockSpec((1, windows, cb), lambda f: (f, 0, 0)),
+            pl.BlockSpec((1, windows, cb), lambda f: (f + bins, 0, 0)),
+        ],
+        out_specs=pl.BlockSpec((1, 2, rb, cb), lambda f: (f, 0, 0, 0)),
+        cost_estimate=pl.CostEstimate(
+            flops=8 * bins * rb * cb * windows,
+            bytes_accessed=2 * (left.size + right.size + bins * 2 * rb * cb),
+            transcendentals=0,
+        ),
+    )(left, left, right, right)
 
 
 def solution(mesh):

time: 146 us -> 141 us (0.966)
  matrix products: 22.7 us -> 7.92 us
  Pallas kernels: 103 us -> 117 us
  local copies, waits for them, and re-layouts: 17 us -> 13.2 us
    dot_general x1 -> x0, matrix products: 14.8 us -> none  [on_device(): jnp.einsum('crwkfi,rcwkfpj->fpij', left, right2, preferred_element_type=j...]
    pallas_call x0 -> x1, Pallas kernels: none -> 14.2 us  [cross(): pl.pallas_call(functools.partial(cross_kernel, scale), out_shape=jax.Shap...]
    convert_element_type x1 -> x0, local copies, waits for them, and re-layouts: 12.2 us -> none  [on_device(): return (cross_sum * (1.0 / total_windows)).astype(jnp.bfloat16)]
    reshape x0 -> x1, local copies, waits for them, and re-layouts: none -> 7.91 us  [on_device(): left = row_block.reshape(windows, 2 * F, rb).transpose(1, 2, 0)]
    transpose x0 -> x1, local copies, waits for them, and re-layouts: none -> 4.07 us  [on_device(): right = col_block.reshape(row_count, col_count, 2 * F, cb).transpose(2, 1...]
    another operation x1 -> x0, local copies, waits for them, and re-layouts: 2.91 us -> none  [on_device(): jnp.stack([right, jnp.stack([right[:, :, :, 1], -right[:, :, :, 0]], axis...]
where the time goes in v2:
time: 141 us
  Pallas kernels  117 us (83%)
  local copies, waits for them, and re-layouts  13.2 us (9%)
  matrix products  7.92 us (6%)
  other arithmetic  2.02 us (1%)
    pallas_call x1, Pallas kernels, exchange(): pl.pallas_call(functools.partial(exchange_kernel, nr, nc), out_shape=(jax...  103 us
    pallas_call x1, Pallas kernels, cross(): pl.pallas_call(functools.partial(cross_kernel, scale), out_shape=jax.Shap...  14.2 us
    reshape x1, local copies, waits for them, and re-layouts, on_device(): left = row_block.reshape(windows, 2 * F, rb).transpose(1, 2, 0)  7.91 us
    dot_general x1, matrix products, one_window(): return jnp.dot(kernel, samples, preferred_element_type=jnp.float32)  7.46 us
    transpose x1, local copies, waits for them, and re-layouts, on_device(): right = col_block.reshape(row_count, col_count, 2 * F, cb).transpose(2, 1...  4.07 us

profile of v2, /device:TPU:54, one launch (start us, length us, event | category | flops | bytes accessed | tf_op | source)
XLA Modules:
  0.0 140.7 jit_solution(7867558307283856726)
XLA Ops:
  0.7 0.7 concatenate.7
  1.3 0.1 subtract_multiply_fusion
  1.4 1.1 cosine_multiply_fusion
  2.5 0.3 tile.10
  2.9 0.1 fusion.12
  3.1 0.5 fusion.2
  3.6 7.5 %fusion = f32[32,4096]{1,0:T(8,128)S(1)} fusion(bf16[1408,4096]{1,0:T(8,128)(2,1)} %param.4, s32[]{:T(128)S(6)} %select_n.25, bf16[32,1408]{1,0:T(8,128)(2,1)S(1)} %bitcast.40), kind=kOutput, calls=%fused_computation | convolution fusion | flops 361758720 | bytes 11952132 | tf_op jit(solution)/shard_map/while/body/eval_jaxpr/dot_general | solution.py:155
  11.1 0.1 fusion.11
  11.2 0.8 fusion.3.w_ref
  11.9 102.5 %shard_map.46 = (bf16[16,8,32,512]{3,2,1,0:T(8,128)(2,1)}, bf16[8,16,32,256]{3,2,1,0:T(8,128)(2,1)}) custom-call(bf16[32,4096]{1,0:T(8,128)(2,1)} %fusion.3.w_ref), custom_call_target="tpu_custom_call" | custom-call | tf_op jit(solution)/shard_map/pallas_call | solution.py:131
  114.5 7.9 %copy.10 = bf16[128,32,512]{0,2,1:T(8,128)(2,1)} copy(bf16[128,32,512]{2,1,0:T(8,128)(2,1)} %bitcast.37) | data formatting | bytes 8388608 | tf_op jit(solution)/shard_map/reshape | solution.py:169
  122.4 4.1 %copy.19 = bf16[32,16,8,256]{3,2,1,0:T(8,128)(2,1)} copy(bf16[32,16,8,256]{3,0,1,2:T(8,128)(2,1)} %bitcast.38) | data formatting | bytes 4194304 | tf_op jit(solution)/shard_map/transpose | solution.py:172
  126.5 14.2 %shard_map.47 = bf16[16,2,512,256]{3,2,1,0:T(8,128)(2,1)} custom-call(bf16[32,512,128]{2,1,0:T(8,128)(2,1)} %bitcast.32, bf16[32,512,128]{2,1,0:T(8,128)(2,1)} %bitcast.33, bf16[32,128,256]{2,1,0:T(8,128)(2,1)} %bitcast.34, bf16[32,128,256]{2,1,0:T(8,128)(2,1)} %bitcast.35), custom_call_target="tpu_custom_call" | custom-call | flops 2147483648 | bytes 14680064 | tf_op jit(solution)/shard_map/pallas_call | solution.py:192
  (6 shorter events, 0.1 us)

commit v3 on v2

--- a/solution.py
+++ b/solution.py
@@ -63,64 +63,85 @@
 MESH = pl.DeviceIdType.MESH
 
 
-def exchange_kernel(nr, nc, w_ref, rbuf, cbuf, r1, c1, r2, c2, s1r, s1c, s2r, s2c, loc):
+def exchange_kernel(nr, nc, w_ref, rbuf, cbuf, r1, c1, r2, c2, sent, loc):
     r = lax.axis_index("row")
     c = lax.axis_index("col")
     rb = rbuf.shape[-1]
     cb = cbuf.shape[-1]
+    nx = nr // 2
+    nz = nc // 4
+    x, y_lo = r // 2, r % 2
+    y_hi, z, core = c // (2 * nz), (c // 2) % nz, c % 2
+    sends = []
+
+    def send(src, dst, recv_sem, device):
+        cp = pltpu.make_async_remote_copy(
+            src_ref=src, dst_ref=dst, send_sem=sent.at[len(sends)], recv_sem=recv_sem,
+            device_id=device, device_id_type=MESH,
+        )
+        cp.start()
+        sends.append(cp)
+
+    def arrived(buf, sem, slot):
+        pltpu.make_async_copy(buf.at[slot], buf.at[slot], sem.at[slot]).wait()
+
     own_r = pltpu.make_async_copy(w_ref.at[:, pl.ds(r * rb, rb)], rbuf.at[c, r], loc.at[0])
     own_r.start()
     own_c = pltpu.make_async_copy(w_ref.at[:, pl.ds(c * cb, cb)], cbuf.at[r, c], loc.at[1])
     own_c.start()
-    sends = []
     for d in range(1, nr):
         t = lax.rem(r + d, nr)
-        cp = pltpu.make_async_remote_copy(
-            src_ref=w_ref.at[:, pl.ds(t * rb, rb)], dst_ref=rbuf.at[c, r],
-            send_sem=s1r.at[d], recv_sem=r1.at[r], device_id=(t, c), device_id_type=MESH,
-        )
-        cp.start()
-        sends.append(cp)
+        send(w_ref.at[:, pl.ds(t * rb, rb)], rbuf.at[c, r], r1.at[r], (t, c))
     for d in range(1, nc):
         t = lax.rem(c + d, nc)
-        cp = pltpu.make_async_remote_copy(
-            src_ref=w_ref.at[:, pl.ds(t * cb, cb)], dst_ref=cbuf.at[r, c],
-            send_sem=s1c.at[d], recv_sem=c1.at[c], device_id=(r, t), device_id_type=MESH,
-        )
-        cp.start()
-        sends.append(cp)
+        send(w_ref.at[:, pl.ds(t * cb, cb)], cbuf.at[r, c], c1.at[c], (r, t))
+
+    def ring_col(hi, dz):
+        return (hi * nz + lax.rem(z + dz, nz)) * 2 + core
+
+    partner_c = ring_col(1 - y_hi, 0)
+    sibling_c = c + 1 - 2 * core
     own_r.wait()
     for d in range(1, nr):
-        src = lax.rem(r + nr - d, nr)
-        pltpu.make_async_copy(rbuf.at[c, src], rbuf.at[c, src], r1.at[src]).wait()
-    for d in range(1, nc):
-        t = lax.rem(c + d, nc)
-        cp = pltpu.make_async_remote_copy(
-            src_ref=rbuf.at[c], dst_ref=rbuf.at[c],
-            send_sem=s2r.at[d], recv_sem=r2.at[c], device_id=(r, t), device_id_type=MESH,
-        )
-        cp.start()
-        sends.append(cp)
+        arrived(rbuf.at[c], r1, lax.rem(r + nr - d, nr))
+    send(rbuf.at[c], rbuf.at[c], r2.at[c], (r, partner_c))
+    send(rbuf.at[c], rbuf.at[c], r2.at[c], (r, sibling_c))
+    for dz in range(1, nz):
+        send(rbuf.at[c], rbuf.at[c], r2.at[c], (r, ring_col(y_hi, dz)))
+
+    def ring_row(lo, dx):
+        return lax.rem(x + dx, nx) * 2 + lo
+
+    partner_r = ring_row(1 - y_lo, 0)
     own_c.wait()
     for d in range(1, nc):
-        src = lax.rem(c + nc - d, nc)
-        pltpu.make_async_copy(cbuf.at[r, src], cbuf.at[r, src], c1.at[src]).wait()
-    for d in range(1, nr):
-        t = lax.rem(r + d, nr)
-        cp = pltpu.make_async_remote_copy(
-            src_ref=cbuf.at[r], dst_ref=cbuf.at[r],
-            send_sem=s2c.at[d], recv_sem=c2.at[r], device_id=(t, c), device_id_type=MESH,
-        )
-        cp.start()
-        sends.append(cp)
+        arrived(cbuf.at[r], c1, lax.rem(c + nc - d, nc))
+    send(cbuf.at[r], cbuf.at[r], c2.at[r], (partner_r, c))
+    for dx in range(1, nx):
+        send(cbuf.at[r], cbuf.at[r], c2.at[r], (ring_row(y_lo, dx), c))
+
+    arrived(rbuf, r2, partner_c)
+    for dz in range(1, nz):
+        send(rbuf.at[partner_c], rbuf.at[partner_c], r2.at[partner_c], (r, ring_col(y_hi, dz)))
+    arrived(cbuf, c2, partner_r)
+    for dx in range(1, nx):
+        send(cbuf.at[partner_r], cbuf.at[partner_r], c2.at[partner_r], (ring_row(y_lo, dx), c))
+
+    send(rbuf.at[partner_c], rbuf.at[partner_c], r2.at[partner_c], (r, sibling_c))
+    for hi in (y_hi, 1 - y_hi):
+        for dz in range(1, nz):
+            slot = ring_col(hi, dz)
+            arrived(rbuf, r2, slot)
+            send(rbuf.at[slot], rbuf.at[slot], r2.at[slot], (r, sibling_c))
+
+    for hi in range(2):
+        for zz in range(nz):
+            arrived(rbuf, r2, (hi * nz + zz) * 2 + 1 - core)
+    for dx in range(1, nx):
+        arrived(cbuf, c2, ring_row(y_lo, dx))
+        arrived(cbuf, c2, ring_row(1 - y_lo, dx))
     for cp in sends:
         cp.wait_send()
-    for d in range(1, nc):
-        src = lax.rem(c + nc - d, nc)
-        pltpu.make_async_copy(rbuf.at[src], rbuf.at[src], r2.at[src]).wait()
-    for d in range(1, nr):
-        src = lax.rem(r + nr - d, nr)
-        pltpu.make_async_copy(cbuf.at[src], cbuf.at[src], c2.at[src]).wait()
 
 
 def exchange(w, nr, nc):
@@ -137,8 +158,7 @@
         in_specs=[pl.BlockSpec(memory_space=pl.ANY)],
         out_specs=(pl.BlockSpec(memory_space=pl.ANY), pl.BlockSpec(memory_space=pl.ANY)),
         scratch_shapes=[
-            dma((nr,)), dma((nc,)), dma((nc,)), dma((nr,)),
-            dma((nr,)), dma((nc,)), dma((nc,)), dma((nr,)), dma((2,)),
+            dma((nr,)), dma((nc,)), dma((nc,)), dma((nr,)), dma((2 * (nr + nc),)), dma((2,)),
         ],
         compiler_params=pltpu.CompilerParams(has_side_effects=True),
     )(w)

time: 141 us -> 87.8 us (0.62)
  the two profiles are of different devices: /device:TPU:54 before, /device:TPU:0 now
where the time goes in v3:
time: 87.8 us; the launch traced here: 86.5 us
  Pallas kernels  62.6 us (71%)
  local copies, waits for them, and re-layouts  13.2 us (15%)
  matrix products  7.92 us (9%)
  other arithmetic  2.02 us (2%)
    pallas_call x1, Pallas kernels, exchange(): pl.pallas_call(functools.partial(exchange_kernel, nr, nc), out_shape=(jax...  48.4 us
    pallas_call x1, Pallas kernels, cross(): pl.pallas_call(functools.partial(cross_kernel, scale), out_shape=jax.Shap...  14.2 us
    reshape x1, local copies, waits for them, and re-layouts, on_device(): left = row_block.reshape(windows, 2 * F, rb).transpose(1, 2, 0)  7.91 us
    dot_general x1, matrix products, one_window(): return jnp.dot(kernel, samples, preferred_element_type=jnp.float32)  7.46 us
    transpose x1, local copies, waits for them, and re-layouts, on_device(): right = col_block.reshape(row_count, col_count, 2 * F, cb).transpose(2, 1...  4.07 us

profile of v3, /device:TPU:0, one launch (start us, length us, event | category | flops | bytes accessed | tf_op | source)
XLA Modules:
  0.0 86.5 jit_solution(4330797020965440447)
XLA Ops:
  0.7 0.7 concatenate.7
  1.3 0.1 subtract_multiply_fusion
  1.4 1.1 %cosine_multiply_fusion = (f32[1,16,1280]{2,1,0:T(8,128)S(1)}, f32[1,16,1280]{2,1,0:T(8,128)S(1)}) fusion(f32[1280]{0:T(1024)S(1)} %subtract_multiply_fusion, s32[16]{0:T(128)} %param.6), kind=kLoop, calls=%fused_computation.30 | loop fusion | flops 245760 | bytes 169024 | tf_op jit(solution)/shard_map/mul | solution.py:26
  2.5 0.3 tile.10
  2.9 0.1 fusion.12
  3.1 0.5 fusion.2
  3.6 7.5 %fusion = f32[32,4096]{1,0:T(8,128)S(1)} fusion(bf16[1408,4096]{1,0:T(8,128)(2,1)} %param.4, s32[]{:T(128)S(6)} %select_n.25, bf16[32,1408]{1,0:T(8,128)(2,1)S(1)} %bitcast.40), kind=kOutput, calls=%fused_computation | convolution fusion | flops 361758720 | bytes 11952132 | tf_op jit(solution)/shard_map/while/body/eval_jaxpr/dot_general | solution.py:175
  11.0 0.1 fusion.11
  11.2 0.8 fusion.3.w_ref
  11.9 48.4 %shard_map.46 = (bf16[16,8,32,512]{3,2,1,0:T(8,128)(2,1)}, bf16[8,16,32,256]{3,2,1,0:T(8,128)(2,1)}) custom-call(bf16[32,4096]{1,0:T(8,128)(2,1)} %fusion.3.w_ref), custom_call_target="tpu_custom_call" | custom-call | tf_op jit(solution)/shard_map/pallas_call | solution.py:152
  60.3 7.9 %copy.10 = bf16[128,32,512]{0,2,1:T(8,128)(2,1)} copy(bf16[128,32,512]{2,1,0:T(8,128)(2,1)} %bitcast.37) | data formatting | bytes 8388608 | tf_op jit(solution)/shard_map/reshape | solution.py:189
  68.3 4.1 %copy.19 = bf16[32,16,8,256]{3,2,1,0:T(8,128)(2,1)} copy(bf16[32,16,8,256]{3,0,1,2:T(8,128)(2,1)} %bitcast.38) | data formatting | bytes 4194304 | tf_op jit(solution)/shard_map/transpose | solution.py:192
  72.3 14.2 %shard_map.47 = bf16[16,2,512,256]{3,2,1,0:T(8,128)(2,1)} custom-call(bf16[32,512,128]{2,1,0:T(8,128)(2,1)} %bitcast.32, bf16[32,512,128]{2,1,0:T(8,128)(2,1)} %bitcast.33, bf16[32,128,256]{2,1,0:T(8,128)(2,1)} %bitcast.34, bf16[32,128,256]{2,1,0:T(8,128)(2,1)} %bitcast.35), custom_call_target="tpu_custom_call" | custom-call | flops 2147483648 | bytes 14680064 | tf_op jit(solution)/shard_map/pallas_call | solution.py:212
  (6 shorter events, 0.1 us)

commit v4 on v3

--- a/solution.py
+++ b/solution.py
@@ -186,7 +186,7 @@
     windows = row_count * col_count * local_count
     rb = channels // row_count
     cb = channels // col_count
-    left = row_block.reshape(windows, 2 * F, rb).transpose(1, 2, 0)
+    left = row_block.reshape(windows, 2 * F, rb).transpose(1, 0, 2)
     right = (
         col_block.reshape(row_count, col_count, 2 * F, cb)
         .transpose(2, 1, 0, 3)
@@ -196,17 +196,24 @@
 
 
 def cross_kernel(scale, l0, l1, r0, r1, out_ref):
-    def dot(a, b):
-        return jnp.dot(a[0], b[0], preferred_element_type=jnp.float32)
-
-    real = dot(l0, r0) + dot(l1, r1)
-    imag = dot(l0, r1) - dot(l1, r0)
-    out_ref[0, 0] = (real * scale).astype(out_ref.dtype)
-    out_ref[0, 1] = (imag * scale).astype(out_ref.dtype)
+    cb = r0.shape[-1]
+    lhs = jnp.concatenate([l0[0], l1[0]], axis=0)
+    rhs = jnp.concatenate(
+        [
+            jnp.concatenate([r0[0], r1[0]], axis=1),
+            jnp.concatenate([r1[0], -r0[0]], axis=1),
+        ],
+        axis=0,
+    )
+    both = lax.dot_general(
+        lhs, rhs, (((0,), (0,)), ((), ())), preferred_element_type=jnp.float32
+    )
+    out_ref[0, 0] = (both[:, :cb] * scale).astype(out_ref.dtype)
+    out_ref[0, 1] = (both[:, cb:] * scale).astype(out_ref.dtype)
 
 
 def cross(left, right, scale):
-    parts, rb, windows = left.shape
+    parts, windows, rb = left.shape
     cb = right.shape[-1]
     bins = parts // 2
     return pl.pallas_call(
@@ -214,8 +221,8 @@
         out_shape=jax.ShapeDtypeStruct((bins, 2, rb, cb), jnp.bfloat16),
         grid=(bins,),
         in_specs=[
-            pl.BlockSpec((1, rb, windows), lambda f: (f, 0, 0)),
-            pl.BlockSpec((1, rb, windows), lambda f: (f + bins, 0, 0)),
+            pl.BlockSpec((1, windows, rb), lambda f: (f, 0, 0)),
+            pl.BlockSpec((1, windows, rb), lambda f: (f + bins, 0, 0)),
             pl.BlockSpec((1, windows, cb), lambda f: (f, 0, 0)),
             pl.BlockSpec((1, windows, cb), lambda f: (f + bins, 0, 0)),
         ],

time: 87.8 us -> 85.5 us (0.974)
  local copies, waits for them, and re-layouts: 13.2 us -> 11.8 us
    reshape x1 -> x0, local copies, waits for them, and re-layouts: 7.91 us -> none  [on_device(): left = row_block.reshape(windows, 2 * F, rb).transpose(1, 2, 0)]
    pallas_call x0 -> x1, local copies, waits for them, and re-layouts: none -> 6.47 us  [exchange(): pl.pallas_call(functools.partial(exchange_kernel, nr, nc), out_shape=(jax...]
where the time goes in v4:
time: 85.5 us; the launch traced here: 84.4 us
  Pallas kernels  61.9 us (72%)
  local copies, waits for them, and re-layouts  11.8 us (14%)
  matrix products  7.92 us (9%)
  other arithmetic  2.02 us (2%)
    pallas_call x1, Pallas kernels, exchange(): pl.pallas_call(functools.partial(exchange_kernel, nr, nc), out_shape=(jax...  48.4 us
    pallas_call x1, Pallas kernels, cross(): pl.pallas_call(functools.partial(cross_kernel, scale), out_shape=jax.Shap...  13.5 us
    dot_general x1, matrix products, one_window(): return jnp.dot(kernel, samples, preferred_element_type=jnp.float32)  7.46 us
    pallas_call x1, local copies, waits for them, and re-layouts, exchange(): pl.pallas_call(functools.partial(exchange_kernel, nr, nc), out_shape=(jax...  6.47 us
    transpose x1, local copies, waits for them, and re-layouts, on_device(): right = col_block.reshape(row_count, col_count, 2 * F, cb).transpose(2, 1...  4.07 us

profile of v4, /device:TPU:0, one launch (start us, length us, event | category | flops | bytes accessed | tf_op | source)
XLA Modules:
  0.0 84.4 jit_solution(10965616686444623096)
XLA Ops:
  0.7 0.7 concatenate.7
  1.3 0.1 subtract_multiply_fusion
  1.4 1.1 %cosine_multiply_fusion = (f32[1,16,1280]{2,1,0:T(8,128)S(1)}, f32[1,16,1280]{2,1,0:T(8,128)S(1)}) fusion(f32[1280]{0:T(1024)S(1)} %subtract_multiply_fusion, s32[16]{0:T(128)} %param.6), kind=kLoop, calls=%fused_computation.31 | loop fusion | flops 245760 | bytes 169024 | tf_op jit(solution)/shard_map/mul | solution.py:26
  2.5 0.3 tile.10
  2.9 0.1 fusion.12
  3.1 0.5 fusion.2
  3.6 7.5 %fusion = f32[32,4096]{1,0:T(8,128)S(1)} fusion(bf16[1408,4096]{1,0:T(8,128)(2,1)} %param.4, s32[]{:T(128)S(6)} %select_n.25, bf16[32,1408]{1,0:T(8,128)(2,1)S(1)} %bitcast.42), kind=kOutput, calls=%fused_computation | convolution fusion | flops 361758720 | bytes 11952132 | tf_op jit(solution)/shard_map/while/body/eval_jaxpr/dot_general | solution.py:175
  11.0 0.1 fusion.11
  11.2 0.8 fusion.3.w_ref
  11.9 48.4 %shard_map.46 = (bf16[16,8,32,512]{3,2,1,0:T(8,128)(2,1)}, bf16[8,16,32,256]{3,2,1,0:T(8,128)(2,1)}) custom-call(bf16[32,4096]{1,0:T(8,128)(2,1)} %fusion.3.w_ref), custom_call_target="tpu_custom_call" | custom-call | tf_op jit(solution)/shard_map/pallas_call | solution.py:152
  60.3 6.5 %copy.20 = bf16[16,8,32,512]{3,1,0,2:T(8,128)(2,1)} copy(bf16[16,8,32,512]{3,2,1,0:T(8,128)(2,1)} %get-tuple-element.20) | data formatting | bytes 8388608 | tf_op jit(solution)/shard_map/pallas_call | solution.py:152
  66.8 4.1 %copy.21 = bf16[32,16,8,256]{3,2,1,0:T(8,128)(2,1)} copy(bf16[32,16,8,256]{3,0,1,2:T(8,128)(2,1)} %bitcast.40) | data formatting | bytes 4194304 | tf_op jit(solution)/shard_map/transpose | solution.py:192
  70.9 13.5 %shard_map.47 = bf16[16,2,512,256]{3,2,1,0:T(8,128)(2,1)} custom-call(bf16[32,128,512]{2,1,0:T(8,128)(2,1)} %bitcast.35, bf16[32,128,512]{2,1,0:T(8,128)(2,1)} %bitcast.36, bf16[32,128,256]{2,1,0:T(8,128)(2,1)} %bitcast.37, bf16[32,128,256]{2,1,0:T(8,128)(2,1)} %bitcast.38), custom_call_target="tpu_custom_call" | custom-call | flops 2147483648 | bytes 14680064 | tf_op jit(solution)/shard_map/pallas_call | solution.py:219
  (6 shorter events, 0.1 us)

commit v5 on v4

--- a/solution.py
+++ b/solution.py
@@ -96,50 +96,63 @@
         t = lax.rem(c + d, nc)
         send(w_ref.at[:, pl.ds(t * cb, cb)], cbuf.at[r, c], c1.at[c], (r, t))
 
-    def ring_col(hi, dz):
-        return (hi * nz + lax.rem(z + dz, nz)) * 2 + core
-
-    partner_c = ring_col(1 - y_hi, 0)
+    step = 1 - 2 * core
+
+    def col_slot(hi, dz):
+        return (hi * nz + lax.rem(z + dz + nz, nz)) * 2 + core
+
+    def row_slot(lo, dx):
+        return lax.rem(x + dx + nx, nx) * 2 + lo
+
     sibling_c = c + 1 - 2 * core
+
+    def to_cols(slot, targets):
+        for t in targets:
+            send(rbuf.at[slot], rbuf.at[slot], r2.at[slot], (r, t))
+
+    def to_rows(slot, targets):
+        for t in targets:
+            send(cbuf.at[slot], cbuf.at[slot], c2.at[slot], (t, c))
+
+    partner_c = col_slot(1 - y_hi, 0)
+    ring_c = [col_slot(y_hi, 1), col_slot(y_hi, -1)]
     own_r.wait()
     for d in range(1, nr):
         arrived(rbuf.at[c], r1, lax.rem(r + nr - d, nr))
-    send(rbuf.at[c], rbuf.at[c], r2.at[c], (r, partner_c))
-    send(rbuf.at[c], rbuf.at[c], r2.at[c], (r, sibling_c))
-    for dz in range(1, nz):
-        send(rbuf.at[c], rbuf.at[c], r2.at[c], (r, ring_col(y_hi, dz)))
-
-    def ring_row(lo, dx):
-        return lax.rem(x + dx, nx) * 2 + lo
-
-    partner_r = ring_row(1 - y_lo, 0)
+    to_cols(c, [partner_c, sibling_c] + ring_c)
+
+    partner_r = row_slot(1 - y_lo, 0)
+    ring_r = [row_slot(y_lo, 1), row_slot(y_lo, -1)]
     own_c.wait()
     for d in range(1, nc):
         arrived(cbuf.at[r], c1, lax.rem(c + nc - d, nc))
-    send(cbuf.at[r], cbuf.at[r], c2.at[r], (partner_r, c))
-    for dx in range(1, nx):
-        send(cbuf.at[r], cbuf.at[r], c2.at[r], (ring_row(y_lo, dx), c))
+    to_rows(r, [partner_r] + ring_r)
 
     arrived(rbuf, r2, partner_c)
-    for dz in range(1, nz):
-        send(rbuf.at[partner_c], rbuf.at[partner_c], r2.at[partner_c], (r, ring_col(y_hi, dz)))
+    to_cols(partner_c, ring_c + [sibling_c])
     arrived(cbuf, c2, partner_r)
-    for dx in range(1, nx):
-        send(cbuf.at[partner_r], cbuf.at[partner_r], c2.at[partner_r], (ring_row(y_lo, dx), c))
-
-    send(rbuf.at[partner_c], rbuf.at[partner_c], r2.at[partner_c], (r, sibling_c))
+    to_rows(partner_r, ring_r)
+
     for hi in (y_hi, 1 - y_hi):
-        for dz in range(1, nz):
-            slot = ring_col(hi, dz)
+        slot = col_slot(hi, -step)
+        arrived(rbuf, r2, slot)
+        to_cols(slot, [col_slot(y_hi, step), sibling_c])
+    for lo in (y_lo, 1 - y_lo):
+        slot = row_slot(lo, -step)
+        arrived(cbuf, c2, slot)
+        to_rows(slot, [row_slot(y_lo, step)])
+    for dz in (1, 2):
+        for hi in (y_hi, 1 - y_hi):
+            slot = col_slot(hi, step * dz)
             arrived(rbuf, r2, slot)
-            send(rbuf.at[slot], rbuf.at[slot], r2.at[slot], (r, sibling_c))
+            to_cols(slot, [sibling_c])
 
     for hi in range(2):
         for zz in range(nz):
             arrived(rbuf, r2, (hi * nz + zz) * 2 + 1 - core)
-    for dx in range(1, nx):
-        arrived(cbuf, c2, ring_row(y_lo, dx))
-        arrived(cbuf, c2, ring_row(1 - y_lo, dx))
+    for dx in (1, 2):
+        for lo in (y_lo, 1 - y_lo):
+            arrived(cbuf, c2, row_slot(lo, step * dx))
     for cp in sends:
         cp.wait_send()
 

time: 85.5 us -> 83.1 us (0.972)
  Pallas kernels: 61.9 us -> 60 us
    pallas_call x1, Pallas kernels: 48.4 us -> 46.5 us  [exchange(): pl.pallas_call(functools.partial(exchange_kernel, nr, nc), out_shape=(jax...]
where the time goes in v5:
time: 83.1 us; the launch traced here: 82.5 us
  Pallas kernels  60 us (72%)
  local copies, waits for them, and re-layouts  11.8 us (14%)
  matrix products  7.92 us (10%)
  other arithmetic  2.02 us (2%)
    pallas_call x1, Pallas kernels, exchange(): pl.pallas_call(functools.partial(exchange_kernel, nr, nc), out_shape=(jax...  46.5 us
    pallas_call x1, Pallas kernels, cross(): pl.pallas_call(functools.partial(cross_kernel, scale), out_shape=jax.Shap...  13.5 us
    dot_general x1, matrix products, one_window(): return jnp.dot(kernel, samples, preferred_element_type=jnp.float32)  7.46 us
    pallas_call x1, local copies, waits for them, and re-layouts, exchange(): pl.pallas_call(functools.partial(exchange_kernel, nr, nc), out_shape=(jax...  6.47 us
    transpose x1, local copies, waits for them, and re-layouts, on_device(): right = col_block.reshape(row_count, col_count, 2 * F, cb).transpose(2, 1...  4.07 us

profile of v5, /device:TPU:0, one launch (start us, length us, event | category | flops | bytes accessed | tf_op | source)
XLA Modules:
  0.0 82.5 jit_solution(477308223268513608)
XLA Ops:
  0.7 0.7 concatenate.7
  1.3 0.1 subtract_multiply_fusion
  1.4 1.1 %cosine_multiply_fusion = (f32[1,16,1280]{2,1,0:T(8,128)S(1)}, f32[1,16,1280]{2,1,0:T(8,128)S(1)}) fusion(f32[1280]{0:T(1024)S(1)} %subtract_multiply_fusion, s32[16]{0:T(128)} %param.6), kind=kLoop, calls=%fused_computation.31 | loop fusion | flops 245760 | bytes 169024 | tf_op jit(solution)/shard_map/mul | solution.py:26
  2.5 0.3 tile.10
  2.9 0.1 fusion.12
  3.1 0.5 fusion.2
  3.6 7.5 %fusion = f32[32,4096]{1,0:T(8,128)S(1)} fusion(bf16[1408,4096]{1,0:T(8,128)(2,1)} %param.4, s32[]{:T(128)S(6)} %select_n.25, bf16[32,1408]{1,0:T(8,128)(2,1)S(1)} %bitcast.42), kind=kOutput, calls=%fused_computation | convolution fusion | flops 361758720 | bytes 11952132 | tf_op jit(solution)/shard_map/while/body/eval_jaxpr/dot_general | solution.py:188
  11.0 0.1 fusion.11
  11.2 0.8 fusion.3.w_ref
  11.9 46.5 %shard_map.46 = (bf16[16,8,32,512]{3,2,1,0:T(8,128)(2,1)}, bf16[8,16,32,256]{3,2,1,0:T(8,128)(2,1)}) custom-call(bf16[32,4096]{1,0:T(8,128)(2,1)} %fusion.3.w_ref), custom_call_target="tpu_custom_call" | custom-call | tf_op jit(solution)/shard_map/pallas_call | solution.py:165
  58.5 6.5 %copy.20 = bf16[16,8,32,512]{3,1,0,2:T(8,128)(2,1)} copy(bf16[16,8,32,512]{3,2,1,0:T(8,128)(2,1)} %get-tuple-element.20) | data formatting | bytes 8388608 | tf_op jit(solution)/shard_map/pallas_call | solution.py:165
  64.9 4.1 %copy.21 = bf16[32,16,8,256]{3,2,1,0:T(8,128)(2,1)} copy(bf16[32,16,8,256]{3,0,1,2:T(8,128)(2,1)} %bitcast.40) | data formatting | bytes 4194304 | tf_op jit(solution)/shard_map/transpose | solution.py:205
  69.0 13.5 %shard_map.47 = bf16[16,2,512,256]{3,2,1,0:T(8,128)(2,1)} custom-call(bf16[32,128,512]{2,1,0:T(8,128)(2,1)} %bitcast.35, bf16[32,128,512]{2,1,0:T(8,128)(2,1)} %bitcast.36, bf16[32,128,256]{2,1,0:T(8,128)(2,1)} %bitcast.37, bf16[32,128,256]{2,1,0:T(8,128)(2,1)} %bitcast.38), custom_call_target="tpu_custom_call" | custom-call | flops 2147483648 | bytes 14680064 | tf_op jit(solution)/shard_map/pallas_call | solution.py:232
  (6 shorter events, 0.1 us)

commit v6 on v5

--- a/solution.py
+++ b/solution.py
@@ -83,18 +83,21 @@
         sends.append(cp)
 
     def arrived(buf, sem, slot):
-        pltpu.make_async_copy(buf.at[slot], buf.at[slot], sem.at[slot]).wait()
+        if buf is cbuf:
+            pltpu.make_async_copy(buf.at[:, slot], buf.at[:, slot], sem.at[slot]).wait()
+        else:
+            pltpu.make_async_copy(buf.at[slot], buf.at[slot], sem.at[slot]).wait()
 
     own_r = pltpu.make_async_copy(w_ref.at[:, pl.ds(r * rb, rb)], rbuf.at[c, r], loc.at[0])
     own_r.start()
-    own_c = pltpu.make_async_copy(w_ref.at[:, pl.ds(c * cb, cb)], cbuf.at[r, c], loc.at[1])
+    own_c = pltpu.make_async_copy(w_ref.at[:, pl.ds(c * cb, cb)], cbuf.at[c, r], loc.at[1])
     own_c.start()
     for d in range(1, nr):
         t = lax.rem(r + d, nr)
         send(w_ref.at[:, pl.ds(t * rb, rb)], rbuf.at[c, r], r1.at[r], (t, c))
     for d in range(1, nc):
         t = lax.rem(c + d, nc)
-        send(w_ref.at[:, pl.ds(t * cb, cb)], cbuf.at[r, c], c1.at[c], (r, t))
+        send(w_ref.at[:, pl.ds(t * cb, cb)], cbuf.at[c, r], c1.at[c], (r, t))
 
     step = 1 - 2 * core
 
@@ -112,7 +115,7 @@
 
     def to_rows(slot, targets):
         for t in targets:
-            send(cbuf.at[slot], cbuf.at[slot], c2.at[slot], (t, c))
+            send(cbuf.at[:, slot], cbuf.at[:, slot], c2.at[slot], (t, c))
 
     partner_c = col_slot(1 - y_hi, 0)
     ring_c = [col_slot(y_hi, 1), col_slot(y_hi, -1)]
@@ -125,7 +128,8 @@
     ring_r = [row_slot(y_lo, 1), row_slot(y_lo, -1)]
     own_c.wait()
     for d in range(1, nc):
-        arrived(cbuf.at[r], c1, lax.rem(c + nc - d, nc))
+        src = lax.rem(c + nc - d, nc)
+        pltpu.make_async_copy(cbuf.at[src, r], cbuf.at[src, r], c1.at[src]).wait()
     to_rows(r, [partner_r] + ring_r)
 
     arrived(rbuf, r2, partner_c)
@@ -166,7 +170,7 @@
         functools.partial(exchange_kernel, nr, nc),
         out_shape=(
             jax.ShapeDtypeStruct((nc, nr, rows, rb), w.dtype),
-            jax.ShapeDtypeStruct((nr, nc, rows, cb), w.dtype),
+            jax.ShapeDtypeStruct((nc, nr, rows, cb), w.dtype),
         ),
         in_specs=[pl.BlockSpec(memory_space=pl.ANY)],
         out_specs=(pl.BlockSpec(memory_space=pl.ANY), pl.BlockSpec(memory_space=pl.ANY)),
@@ -199,24 +203,27 @@
     windows = row_count * col_count * local_count
     rb = channels // row_count
     cb = channels // col_count
-    left = row_block.reshape(windows, 2 * F, rb).transpose(1, 0, 2)
-    right = (
-        col_block.reshape(row_count, col_count, 2 * F, cb)
-        .transpose(2, 1, 0, 3)
-        .reshape(2 * F, windows, cb)
-    )
+    left = row_block.reshape(windows, 2 * F, rb)
+    right = col_block.reshape(windows, 2 * F, cb)
     return cross(left, right, 1.0 / total_windows)
 
 
-def cross_kernel(scale, l0, l1, r0, r1, out_ref):
-    cb = r0.shape[-1]
-    lhs = jnp.concatenate([l0[0], l1[0]], axis=0)
+def cross_kernel(scale, l_ref, r_ref, out_ref):
+    f = pl.program_id(0)
+    for fixed in range(l_ref.shape[1] // 2):
+
+        @pl.when(f == fixed)
+        def _():
+            one_bin(scale, fixed, l_ref.shape[1] // 2, l_ref, r_ref, out_ref)
+
+
+def one_bin(scale, f, bins, l_ref, r_ref, out_ref):
+    cb = r_ref.shape[-1]
+    l0, l1 = l_ref[:, f, :], l_ref[:, f + bins, :]
+    r0, r1 = r_ref[:, f, :], r_ref[:, f + bins, :]
+    lhs = jnp.concatenate([l0, l1], axis=0)
     rhs = jnp.concatenate(
-        [
-            jnp.concatenate([r0[0], r1[0]], axis=1),
-            jnp.concatenate([r1[0], -r0[0]], axis=1),
-        ],
-        axis=0,
+        [jnp.concatenate([r0, r1], axis=1), jnp.concatenate([r1, -r0], axis=1)], axis=0
     )
     both = lax.dot_general(
         lhs, rhs, (((0,), (0,)), ((), ())), preferred_element_type=jnp.float32
@@ -226,7 +233,7 @@
 
 
 def cross(left, right, scale):
-    parts, windows, rb = left.shape
+    windows, parts, rb = left.shape
     cb = right.shape[-1]
     bins = parts // 2
     return pl.pallas_call(
@@ -234,10 +241,8 @@
         out_shape=jax.ShapeDtypeStruct((bins, 2, rb, cb), jnp.bfloat16),
         grid=(bins,),
         in_specs=[
-            pl.BlockSpec((1, windows, rb), lambda f: (f, 0, 0)),
-            pl.BlockSpec((1, windows, rb), lambda f: (f + bins, 0, 0)),
-            pl.BlockSpec((1, windows, cb), lambda f: (f, 0, 0)),
-            pl.BlockSpec((1, windows, cb), lambda f: (f + bins, 0, 0)),
+            pl.BlockSpec((windows, parts, rb), lambda f: (0, 0, 0)),
+            pl.BlockSpec((windows, parts, cb), lambda f: (0, 0, 0)),
         ],
         out_specs=pl.BlockSpec((1, 2, rb, cb), lambda f: (f, 0, 0, 0)),
         cost_estimate=pl.CostEstimate(
@@ -245,7 +250,7 @@
             bytes_accessed=2 * (left.size + right.size + bins * 2 * rb * cb),
             transcendentals=0,
         ),
-    )(left, left, right, right)
+    )(left, right)
 
 
 def solution(mesh):

time: 83.1 us -> 81 us (0.975)
  local copies, waits for them, and re-layouts: 11.8 us -> 1.25 us
  Pallas kernels: 60 us -> 68.9 us
    pallas_call x1, Pallas kernels: 13.5 us -> 22.3 us  [cross(): pl.pallas_call(functools.partial(cross_kernel, scale), out_shape=jax.Shap...]
    pallas_call x1 -> x0, local copies, waits for them, and re-layouts: 6.47 us -> none  [exchange(): pl.pallas_call(functools.partial(exchange_kernel, nr, nc), out_shape=(jax...]
    transpose x1 -> x0, local copies, waits for them, and re-layouts: 4.07 us -> none  [on_device(): right = col_block.reshape(row_count, col_count, 2 * F, cb).transpose(2, 1...]
where the time goes in v6:
time: 81 us; the launch traced here: 80.8 us
  Pallas kernels  68.9 us (85%)
  matrix products  7.91 us (10%)
  other arithmetic  2.02 us (2%)
  local copies, waits for them, and re-layouts  1.25 us (2%)
    pallas_call x1, Pallas kernels, exchange(): pl.pallas_call(functools.partial(exchange_kernel, nr, nc), out_shape=(jax...  46.5 us
    pallas_call x1, Pallas kernels, cross(): pl.pallas_call(functools.partial(cross_kernel, scale), out_shape=jax.Shap...  22.3 us
    dot_general x1, matrix products, one_window(): return jnp.dot(kernel, samples, preferred_element_type=jnp.float32)  7.46 us

profile of v6, /device:TPU:0, one launch (start us, length us, event | category | flops | bytes accessed | tf_op | source)
XLA Modules:
  0.0 80.8 jit_solution(6778523443988265984)
XLA Ops:
  0.7 0.7 concatenate.7
  1.3 0.1 subtract_multiply_fusion
  1.4 1.1 %cosine_multiply_fusion = (f32[1,16,1280]{2,1,0:T(8,128)S(1)}, f32[1,16,1280]{2,1,0:T(8,128)S(1)}) fusion(f32[1280]{0:T(1024)S(1)} %subtract_multiply_fusion, s32[16]{0:T(128)} %param.6), kind=kLoop, calls=%fused_computation.29 | loop fusion | flops 245760 | bytes 169024 | tf_op jit(solution)/shard_map/mul | solution.py:26
  2.5 0.3 tile.10
  2.9 0.1 fusion.12
  3.1 0.5 fusion.2
  3.6 7.5 %fusion = f32[32,4096]{1,0:T(8,128)S(1)} fusion(bf16[1408,4096]{1,0:T(8,128)(2,1)} %param.4, s32[]{:T(128)S(6)} %select_n.25, bf16[32,1408]{1,0:T(8,128)(2,1)S(1)} %bitcast.32), kind=kOutput, calls=%fused_computation | convolution fusion | flops 361758720 | bytes 11952132 | tf_op jit(solution)/shard_map/while/body/eval_jaxpr/dot_general | solution.py:192
  11.0 0.1 fusion.11
  11.2 0.8 fusion.3.w_ref
  11.9 46.5 %shard_map.46 = (bf16[16,8,32,512]{3,2,1,0:T(8,128)(2,1)}, bf16[16,8,32,256]{3,2,1,0:T(8,128)(2,1)}) custom-call(bf16[32,4096]{1,0:T(8,128)(2,1)} %fusion.3.w_ref), custom_call_target="tpu_custom_call" | custom-call | tf_op jit(solution)/shard_map/pallas_call | solution.py:169
  58.5 22.3 %shard_map.47 = bf16[16,2,512,256]{3,2,1,0:T(8,128)(2,1)} custom-call(bf16[128,32,512]{2,1,0:T(8,128)(2,1)} %bitcast.29, bf16[128,32,256]{2,1,0:T(8,128)(2,1)} %bitcast.30), custom_call_target="tpu_custom_call" | custom-call | flops 2147483648 | bytes 14680064 | tf_op jit(solution)/shard_map/pallas_call | solution.py:239
  (6 shorter events, 0.1 us)

commit v7 on v6

--- a/solution.py
+++ b/solution.py
@@ -208,19 +208,18 @@
     return cross(left, right, 1.0 / total_windows)
 
 
-def cross_kernel(scale, l_ref, r_ref, out_ref):
+def cross_kernel(scale, l_ref, r_ref, out_ref, lt, rt):
     f = pl.program_id(0)
-    for fixed in range(l_ref.shape[1] // 2):
-
-        @pl.when(f == fixed)
-        def _():
-            one_bin(scale, fixed, l_ref.shape[1] // 2, l_ref, r_ref, out_ref)
-
-
-def one_bin(scale, f, bins, l_ref, r_ref, out_ref):
+    bins = pl.num_programs(0)
     cb = r_ref.shape[-1]
-    l0, l1 = l_ref[:, f, :], l_ref[:, f + bins, :]
-    r0, r1 = r_ref[:, f, :], r_ref[:, f + bins, :]
+
+    @pl.when(f == 0)
+    def _():
+        lt[...] = pltpu.einshape("nkc->knc", l_ref[...])
+        rt[...] = pltpu.einshape("nkc->knc", r_ref[...])
+
+    l0, l1 = lt[f], lt[f + bins]
+    r0, r1 = rt[f], rt[f + bins]
     lhs = jnp.concatenate([l0, l1], axis=0)
     rhs = jnp.concatenate(
         [jnp.concatenate([r0, r1], axis=1), jnp.concatenate([r1, -r0], axis=1)], axis=0
@@ -245,6 +244,10 @@
             pl.BlockSpec((windows, parts, cb), lambda f: (0, 0, 0)),
         ],
         out_specs=pl.BlockSpec((1, 2, rb, cb), lambda f: (f, 0, 0, 0)),
+        scratch_shapes=[
+            pltpu.VMEM((parts, windows, rb), left.dtype),
+            pltpu.VMEM((parts, windows, cb), right.dtype),
+        ],
         cost_estimate=pl.CostEstimate(
             flops=8 * bins * rb * cb * windows,
             bytes_accessed=2 * (left.size + right.size + bins * 2 * rb * cb),

time: 81 us -> 72.5 us (0.90)
  Pallas kernels: 68.9 us -> 60.4 us
    pallas_call x1, Pallas kernels: 22.3 us -> 13.8 us  [cross(): pl.pallas_call(functools.partial(cross_kernel, scale), out_shape=jax.Shap...]
where the time goes in v7:
time: 72.5 us; the launch traced here: 72.3 us
  Pallas kernels  60.4 us (83%)
  matrix products  7.92 us (11%)
  other arithmetic  2.02 us (3%)
  local copies, waits for them, and re-layouts  1.25 us (2%)
  between operations  0.75 us (1%)
    pallas_call x1, Pallas kernels, exchange(): pl.pallas_call(functools.partial(exchange_kernel, nr, nc), out_shape=(jax...  46.5 us
    pallas_call x1, Pallas kernels, cross(): pl.pallas_call(functools.partial(cross_kernel, scale), out_shape=jax.Shap...  13.8 us
    dot_general x1, matrix products, one_window(): return jnp.dot(kernel, samples, preferred_element_type=jnp.float32)  7.46 us

profile of v7, /device:TPU:0, one launch (start us, length us, event | category | flops | bytes accessed | tf_op | source)
XLA Modules:
  0.0 72.3 jit_solution(7433485325187925627)
XLA Ops:
  0.7 0.7 concatenate.7
  1.3 0.1 subtract_multiply_fusion
  1.4 1.1 %cosine_multiply_fusion = (f32[1,16,1280]{2,1,0:T(8,128)S(1)}, f32[1,16,1280]{2,1,0:T(8,128)S(1)}) fusion(f32[1280]{0:T(1024)S(1)} %subtract_multiply_fusion, s32[16]{0:T(128)} %param.6), kind=kLoop, calls=%fused_computation.29 | loop fusion | flops 245760 | bytes 169024 | tf_op jit(solution)/shard_map/mul | solution.py:26
  2.5 0.3 tile.10
  2.9 0.1 fusion.12
  3.1 0.5 fusion.2
  3.6 7.5 %fusion = f32[32,4096]{1,0:T(8,128)S(1)} fusion(bf16[1408,4096]{1,0:T(8,128)(2,1)} %param.4, s32[]{:T(128)S(6)} %select_n.25, bf16[32,1408]{1,0:T(8,128)(2,1)S(1)} %bitcast.32), kind=kOutput, calls=%fused_computation | convolution fusion | flops 361758720 | bytes 11952132 | tf_op jit(solution)/shard_map/while/body/eval_jaxpr/dot_general | solution.py:192
  11.0 0.1 fusion.11
  11.2 0.8 %fusion.3.w_ref = bf16[32,4096]{1,0:T(8,128)(2,1)} fusion(f32[32,4096]{1,0:T(8,128)S(1)} %fusion, f32[16,4096]{1,0:T(8,128)S(1)} %fusion.11), kind=kLoop, calls=%fused_computation.5 | loop fusion | flops 262144 | bytes 1048576 | tf_op jit(solution)/shard_map/convert_element_type | solution.py:60
  11.9 46.5 %shard_map.46 = (bf16[16,8,32,512]{3,2,1,0:T(8,128)(2,1)}, bf16[16,8,32,256]{3,2,1,0:T(8,128)(2,1)}) custom-call(bf16[32,4096]{1,0:T(8,128)(2,1)} %fusion.3.w_ref), custom_call_target="tpu_custom_call" | custom-call | tf_op jit(solution)/shard_map/pallas_call | solution.py:169
  58.5 13.8 %shard_map.47 = bf16[16,2,512,256]{3,2,1,0:T(8,128)(2,1)} custom-call(bf16[128,32,512]{2,1,0:T(8,128)(2,1)} %bitcast.29, bf16[128,32,256]{2,1,0:T(8,128)(2,1)} %bitcast.30), custom_call_target="tpu_custom_call" | custom-call | flops 2147483648 | bytes 14680064 | tf_op jit(solution)/shard_map/pallas_call | solution.py:238
  (6 shorter events, 0.1 us)

commit v8 on v7

--- a/solution.py
+++ b/solution.py
@@ -23,9 +23,9 @@
     angles = 2.0 * math.pi / WL * phase_index.astype(jnp.float32)
     centre = (jnp.arange(WL, dtype=jnp.float32) + 0.5) / WL
     window_taper = (0.5 - 0.5 * jnp.cos(2.0 * math.pi * centre)) / math.sqrt(WL)
-    pattern = jnp.stack([jnp.cos(angles) * window_taper, -jnp.sin(angles) * window_taper]).reshape(
-        2 * F, WL
-    )
+    pattern = jnp.stack(
+        [jnp.cos(angles) * window_taper, -jnp.sin(angles) * window_taper], axis=1
+    ).reshape(2 * F, WL)
     lanes = 128
     blocks = pl_cdiv(span, lanes)
     width = 2 * lanes
@@ -54,10 +54,10 @@
 
 
 def whiten(spectra):
-    shaped = spectra.reshape(spectra.shape[0], 2, F, spectra.shape[-1])
-    magnitude = jnp.sqrt(shaped[:, 0] * shaped[:, 0] + shaped[:, 1] * shaped[:, 1])
+    shaped = spectra.reshape(spectra.shape[0], F, 2, spectra.shape[-1])
+    magnitude = jnp.sqrt(shaped[:, :, 0] * shaped[:, :, 0] + shaped[:, :, 1] * shaped[:, :, 1])
     inverse = 1.0 / jnp.maximum(magnitude, floor_level)
-    return (shaped * inverse[:, None]).astype(jnp.bfloat16)
+    return (shaped * inverse[:, :, None]).astype(jnp.bfloat16)
 
 
 MESH = pl.DeviceIdType.MESH
@@ -208,18 +208,18 @@
     return cross(left, right, 1.0 / total_windows)
 
 
-def cross_kernel(scale, l_ref, r_ref, out_ref, lt, rt):
+def cross_kernel(scale, group, l_ref, r_ref, out_ref, lt, rt):
     f = pl.program_id(0)
-    bins = pl.num_programs(0)
     cb = r_ref.shape[-1]
-
-    @pl.when(f == 0)
+    within = lax.rem(f, group)
+
+    @pl.when(within == 0)
     def _():
         lt[...] = pltpu.einshape("nkc->knc", l_ref[...])
         rt[...] = pltpu.einshape("nkc->knc", r_ref[...])
 
-    l0, l1 = lt[f], lt[f + bins]
-    r0, r1 = rt[f], rt[f + bins]
+    l0, l1 = lt[2 * within], lt[2 * within + 1]
+    r0, r1 = rt[2 * within], rt[2 * within + 1]
     lhs = jnp.concatenate([l0, l1], axis=0)
     rhs = jnp.concatenate(
         [jnp.concatenate([r0, r1], axis=1), jnp.concatenate([r1, -r0], axis=1)], axis=0
@@ -235,18 +235,20 @@
     windows, parts, rb = left.shape
     cb = right.shape[-1]
     bins = parts // 2
+    group = 4
+    rows = 2 * group
     return pl.pallas_call(
-        functools.partial(cross_kernel, scale),
+        functools.partial(cross_kernel, scale, group),
         out_shape=jax.ShapeDtypeStruct((bins, 2, rb, cb), jnp.bfloat16),
         grid=(bins,),
         in_specs=[
-            pl.BlockSpec((windows, parts, rb), lambda f: (0, 0, 0)),
-            pl.BlockSpec((windows, parts, cb), lambda f: (0, 0, 0)),
+            pl.BlockSpec((windows, rows, rb), lambda f: (0, f // group, 0)),
+            pl.BlockSpec((windows, rows, cb), lambda f: (0, f // group, 0)),
         ],
         out_specs=pl.BlockSpec((1, 2, rb, cb), lambda f: (f, 0, 0, 0)),
         scratch_shapes=[
-            pltpu.VMEM((parts, windows, rb), left.dtype),
-            pltpu.VMEM((parts, windows, cb), right.dtype),
+            pltpu.VMEM((rows, windows, rb), left.dtype),
+            pltpu.VMEM((rows, windows, cb), right.dtype),
         ],
         cost_estimate=pl.CostEstimate(
             flops=8 * bins * rb * cb * windows,

time: 72.5 us -> 76.1 us (1.050)
  local copies, waits for them, and re-layouts: 1.25 us -> 2.98 us
  Pallas kernels: 60.4 us -> 61.8 us
    pallas_call x1, Pallas kernels: 13.8 us -> 15.3 us  [cross(): pl.pallas_call(functools.partial(cross_kernel, scale, group), out_shape=j...]
where the time goes in v8:
time: 76.1 us; the launch traced here: 75.8 us
  Pallas kernels  61.8 us (81%)
  matrix products  7.92 us (10%)
  local copies, waits for them, and re-layouts  2.98 us (4%)
  other arithmetic  2.25 us (3%)
  between operations  0.79 us (1%)
    pallas_call x1, Pallas kernels, exchange(): pl.pallas_call(functools.partial(exchange_kernel, nr, nc), out_shape=(jax...  46.5 us
    pallas_call x1, Pallas kernels, cross(): pl.pallas_call(functools.partial(cross_kernel, scale, group), out_shape=j...  15.3 us
    dot_general x1, matrix products, one_window(): return jnp.dot(kernel, samples, preferred_element_type=jnp.float32)  7.46 us

profile of v8, /device:TPU:0, one launch (start us, length us, event | category | flops | bytes accessed | tf_op | source)
XLA Modules:
  0.0 75.8 jit_solution(8888796274968373031)
XLA Ops:
  0.7 0.7 concatenate.7
  1.3 0.1 subtract_multiply_fusion
  1.4 1.1 %cosine_multiply_fusion = (f32[16,1,1280]{2,0,1:T(8,128)S(1)}, f32[16,1,1280]{2,0,1:T(8,128)S(1)}) fusion(f32[1280]{0:T(1024)S(1)} %subtract_multiply_fusion, s32[16]{0:T(128)} %param.6), kind=kLoop, calls=%fused_computation.28 | loop fusion | flops 245760 | bytes 169024 | tf_op jit(solution)/shard_map/mul | solution.py:27
  2.5 0.1 copy.11
  2.6 0.1 reshape.175
  2.8 0.3 tile.10
  3.2 0.1 fusion.11
  3.4 0.5 fusion.2
  3.9 7.5 %fusion = f32[32,4096]{1,0:T(8,128)S(1)} fusion(bf16[1408,4096]{1,0:T(8,128)(2,1)} %param.4, s32[]{:T(128)S(6)} %select_n.25, bf16[32,1408]{1,0:T(8,128)(2,1)S(1)} %bitcast.24), kind=kOutput, calls=%fused_computation | convolution fusion | flops 361758720 | bytes 11952132 | tf_op jit(solution)/shard_map/while/body/eval_jaxpr/dot_general | solution.py:192
  11.3 0.3 reshape.180
  11.6 0.6 fusion.21
  12.2 0.3 fusion.10
  12.5 0.3 mul.135
  12.8 0.4 mul.136
  13.2 0.8 multiply_convert_fusion.w_ref
  13.9 46.5 %shard_map.46 = (bf16[16,8,32,512]{3,2,1,0:T(8,128)(2,1)}, bf16[16,8,32,256]{3,2,1,0:T(8,128)(2,1)}) custom-call(bf16[32,4096]{1,0:T(8,128)(2,1)} %multiply_convert_fusion.w_ref), custom_call_target="tpu_custom_call" | custom-call | tf_op jit(solution)/shard_map/pallas_call | solution.py:169
  60.5 15.3 %shard_map.47 = bf16[16,2,512,256]{3,2,1,0:T(8,128)(2,1)} custom-call(bf16[128,32,512]{2,1,0:T(8,128)(2,1)} %bitcast.22, bf16[128,32,256]{2,1,0:T(8,128)(2,1)} %bitcast.23), custom_call_target="tpu_custom_call" | custom-call | flops 2147483648 | bytes 14680064 | tf_op jit(solution)/shard_map/pallas_call | solution.py:240
  (6 shorter events, 0.1 us)

commit v9 on v7

--- a/solution.py
+++ b/solution.py
@@ -186,12 +186,11 @@
     span = WL + TAPS - 1
     local_count = offsets.shape[0]
 
-    def one_window(window):
-        first_row = window * WL + offsets[window]
-        samples = lax.dynamic_slice_in_dim(record, first_row, span, 0)
-        return jnp.dot(kernel, samples, preferred_element_type=jnp.float32)
-
-    spectra = lax.map(one_window, jnp.arange(local_count, dtype=jnp.int32))
+    assert local_count == 1
+    placed = lax.dynamic_update_slice(
+        jnp.zeros((kernel.shape[0], record.shape[0]), kernel.dtype), kernel, (0, offsets[0])
+    )
+    spectra = jnp.dot(placed, record, preferred_element_type=jnp.float32)[None]
     whitened = whiten(spectra)
     channels = whitened.shape[-1]
     row_count = lax.axis_size("row")

time: 72.5 us -> 72.2 us (level)
  matrix products: 7.92 us -> 6.82 us
  local copies, waits for them, and re-layouts: 1.25 us -> 2.06 us
    dot_general x1, matrix products: 7.46 us -> 6.36 us  [on_device(): spectra = jnp.dot(placed, record, preferred_element_type=jnp.float32)[None]]
    dynamic_update_slice x0 -> x1, local copies, waits for them, and re-layouts: none -> 0.8 us  [on_device(): lax.dynamic_update_slice(jnp.zeros((kernel.shape[0], record.shape[0]), ke...]
where the time goes in v9:
time: 72.2 us; the launch traced here: 72 us
  Pallas kernels  60.4 us (84%)
  matrix products  6.82 us (9%)
  local copies, waits for them, and re-layouts  2.06 us (3%)
  other arithmetic  2.02 us (3%)
  between operations  0.76 us (1%)
    pallas_call x1, Pallas kernels, exchange(): pl.pallas_call(functools.partial(exchange_kernel, nr, nc), out_shape=(jax...  46.5 us
    pallas_call x1, Pallas kernels, cross(): pl.pallas_call(functools.partial(cross_kernel, scale), out_shape=jax.Shap...  13.8 us
    dot_general x1, matrix products, on_device(): spectra = jnp.dot(placed, record, preferred_element_type=jnp.float32)[None]  6.36 us

profile of v9, /device:TPU:0, one launch (start us, length us, event | category | flops | bytes accessed | tf_op | source)
XLA Modules:
  0.0 72.0 jit_solution(17819297383635033318)
XLA Ops:
  0.7 0.7 concatenate.7
  1.3 0.1 subtract_multiply_fusion
  1.4 1.1 %cosine_multiply_fusion = (f32[1,16,1280]{2,1,0:T(8,128)S(1)}, f32[1,16,1280]{2,1,0:T(8,128)S(1)}) fusion(f32[1280]{0:T(1024)S(1)} %subtract_multiply_fusion, s32[16]{0:T(128)} %param.6), kind=kLoop, calls=%fused_computation.26 | loop fusion | flops 245760 | bytes 169024 | tf_op jit(solution)/shard_map/mul | solution.py:26
  2.5 0.3 tile.10
  2.9 0.1 fusion.10
  3.1 0.5 fusion
  3.6 0.8 %dynamic_update_slice.3 = bf16[32,1408]{1,0:T(8,128)(2,1)S(1)} dynamic-update-slice(bf16[32,1408]{1,0:T(8,128)(2,1)S(1)} %broadcast_in_dim.2, bf16[32,1380]{1,0:T(8,128)(2,1)S(1)} %bitcast.35, s32[]{:T(128)} %constant.12.clone.1, s32[]{:T(128)S(6)} %select_n.22) | dynamic-update-slice | bytes 176644 | tf_op jit(solution)/shard_map/dynamic_update_slice | solution.py:190
  4.4 6.4 %fusion.18 = f32[32,4096]{1,0:T(8,128)S(1)} fusion(bf16[32,1408]{1,0:T(8,128)(2,1)S(1)} %dynamic_update_slice.3, bf16[1408,4096]{1,0:T(8,128)(2,1)} %param.4), kind=kOutput, calls=%fused_computation.33 | convolution fusion | flops 369098752 | bytes 12148736 | tf_op jit(solution)/shard_map/dot_general | solution.py:193
  10.8 0.1 fusion.9
  10.9 0.7 %fusion.1.w_ref = bf16[32,4096]{1,0:T(8,128)(2,1)} fusion(f32[32,4096]{1,0:T(8,128)S(1)} %fusion.18, f32[16,4096]{1,0:T(8,128)S(1)} %fusion.9), kind=kLoop, calls=%fused_computation.3 | loop fusion | flops 262144 | bytes 1048576 | tf_op jit(solution)/shard_map/convert_element_type | solution.py:60
  11.7 46.5 %shard_map.46 = (bf16[16,8,32,512]{3,2,1,0:T(8,128)(2,1)}, bf16[16,8,32,256]{3,2,1,0:T(8,128)(2,1)}) custom-call(bf16[32,4096]{1,0:T(8,128)(2,1)} %fusion.1.w_ref), custom_call_target="tpu_custom_call" | custom-call | tf_op jit(solution)/shard_map/pallas_call | solution.py:169
  58.2 13.8 %shard_map.47 = bf16[16,2,512,256]{3,2,1,0:T(8,128)(2,1)} custom-call(bf16[128,32,512]{2,1,0:T(8,128)(2,1)} %bitcast.32, bf16[128,32,256]{2,1,0:T(8,128)(2,1)} %bitcast.33), custom_call_target="tpu_custom_call" | custom-call | flops 2147483648 | bytes 14680064 | tf_op jit(solution)/shard_map/pallas_call | solution.py:237
  (7 shorter events, 0.1 us)

commit v10 on v9

--- a/solution.py
+++ b/solution.py
@@ -207,15 +207,27 @@
     return cross(left, right, 1.0 / total_windows)
 
 
-def cross_kernel(scale, l_ref, r_ref, out_ref, lt, rt):
+def cross_kernel(scale, chunks, l_hbm, r_hbm, out_ref, l_in, r_in, lt, rt, sems):
     f = pl.program_id(0)
     bins = pl.num_programs(0)
-    cb = r_ref.shape[-1]
+    cb = r_hbm.shape[-1]
+    size = l_hbm.shape[0] // chunks
 
     @pl.when(f == 0)
     def _():
-        lt[...] = pltpu.einshape("nkc->knc", l_ref[...])
-        rt[...] = pltpu.einshape("nkc->knc", r_ref[...])
+        copies = []
+        for i in range(chunks):
+            part = pl.ds(i * size, size)
+            for j, (src, dst) in enumerate(((l_hbm, l_in), (r_hbm, r_in))):
+                cp = pltpu.make_async_copy(src.at[part], dst.at[part], sems.at[j, i])
+                cp.start()
+                copies.append(cp)
+        for i in range(chunks):
+            part = pl.ds(i * size, size)
+            copies[2 * i].wait()
+            lt[:, part, :] = pltpu.einshape("nkc->knc", l_in[part])
+            copies[2 * i + 1].wait()
+            rt[:, part, :] = pltpu.einshape("nkc->knc", r_in[part])
 
     l0, l1 = lt[f], lt[f + bins]
     r0, r1 = rt[f], rt[f + bins]
@@ -234,18 +246,19 @@
     windows, parts, rb = left.shape
     cb = right.shape[-1]
     bins = parts // 2
+    chunks = 8
     return pl.pallas_call(
-        functools.partial(cross_kernel, scale),
+        functools.partial(cross_kernel, scale, chunks),
         out_shape=jax.ShapeDtypeStruct((bins, 2, rb, cb), jnp.bfloat16),
         grid=(bins,),
-        in_specs=[
-            pl.BlockSpec((windows, parts, rb), lambda f: (0, 0, 0)),
-            pl.BlockSpec((windows, parts, cb), lambda f: (0, 0, 0)),
-        ],
+        in_specs=[pl.BlockSpec(memory_space=pl.ANY), pl.BlockSpec(memory_space=pl.ANY)],
         out_specs=pl.BlockSpec((1, 2, rb, cb), lambda f: (f, 0, 0, 0)),
         scratch_shapes=[
+            pltpu.VMEM((windows, parts, rb), left.dtype),
+            pltpu.VMEM((windows, parts, cb), right.dtype),
             pltpu.VMEM((parts, windows, rb), left.dtype),
             pltpu.VMEM((parts, windows, cb), right.dtype),
+            pltpu.SemaphoreType.DMA((2, chunks)),
         ],
         cost_estimate=pl.CostEstimate(
             flops=8 * bins * rb * cb * windows,

time: 72.2 us -> 70.7 us (0.979)
  Pallas kernels: 60.4 us -> 58.8 us
    pallas_call x1, Pallas kernels: 13.8 us -> 12.3 us  [cross(): pl.pallas_call(functools.partial(cross_kernel, scale, chunks), out_shape=...]
where the time goes in v10:
time: 70.7 us; the launch traced here: 70.5 us
  Pallas kernels  58.8 us (83%)
  matrix products  6.82 us (10%)
  local copies, waits for them, and re-layouts  2.06 us (3%)
  other arithmetic  2.02 us (3%)
  between operations  0.76 us (1%)
    pallas_call x1, Pallas kernels, exchange(): pl.pallas_call(functools.partial(exchange_kernel, nr, nc), out_shape=(jax...  46.5 us
    pallas_call x1, Pallas kernels, cross(): pl.pallas_call(functools.partial(cross_kernel, scale, chunks), out_shape=...  12.3 us
    dot_general x1, matrix products, on_device(): spectra = jnp.dot(placed, record, preferred_element_type=jnp.float32)[None]  6.36 us

profile of v10, /device:TPU:0, one launch (start us, length us, event | category | flops | bytes accessed | tf_op | source)
XLA Modules:
  0.0 70.5 jit_solution(5898852508386011255)
XLA Ops:
  0.7 0.7 concatenate.7
  1.3 0.1 subtract_multiply_fusion
  1.4 1.1 %cosine_multiply_fusion = (f32[1,16,1280]{2,1,0:T(8,128)S(1)}, f32[1,16,1280]{2,1,0:T(8,128)S(1)}) fusion(f32[1280]{0:T(1024)S(1)} %subtract_multiply_fusion, s32[16]{0:T(128)} %param.6), kind=kLoop, calls=%fused_computation.26 | loop fusion | flops 245760 | bytes 169024 | tf_op jit(solution)/shard_map/mul | solution.py:26
  2.5 0.3 tile.10
  2.9 0.1 fusion.10
  3.1 0.5 fusion
  3.6 0.8 %dynamic_update_slice.3 = bf16[32,1408]{1,0:T(8,128)(2,1)S(1)} dynamic-update-slice(bf16[32,1408]{1,0:T(8,128)(2,1)S(1)} %broadcast_in_dim.2, bf16[32,1380]{1,0:T(8,128)(2,1)S(1)} %bitcast.35, s32[]{:T(128)} %constant.12.clone.1, s32[]{:T(128)S(6)} %select_n.22) | dynamic-update-slice | bytes 176644 | tf_op jit(solution)/shard_map/dynamic_update_slice | solution.py:190
  4.4 6.4 %fusion.18 = f32[32,4096]{1,0:T(8,128)S(1)} fusion(bf16[32,1408]{1,0:T(8,128)(2,1)S(1)} %dynamic_update_slice.3, bf16[1408,4096]{1,0:T(8,128)(2,1)} %param.4), kind=kOutput, calls=%fused_computation.33 | convolution fusion | flops 369098752 | bytes 12148736 | tf_op jit(solution)/shard_map/dot_general | solution.py:193
  10.8 0.1 fusion.9
  10.9 0.7 %fusion.1.w_ref = bf16[32,4096]{1,0:T(8,128)(2,1)} fusion(f32[32,4096]{1,0:T(8,128)S(1)} %fusion.18, f32[16,4096]{1,0:T(8,128)S(1)} %fusion.9), kind=kLoop, calls=%fused_computation.3 | loop fusion | flops 262144 | bytes 1048576 | tf_op jit(solution)/shard_map/convert_element_type | solution.py:60
  11.7 46.5 %shard_map.46 = (bf16[16,8,32,512]{3,2,1,0:T(8,128)(2,1)}, bf16[16,8,32,256]{3,2,1,0:T(8,128)(2,1)}) custom-call(bf16[32,4096]{1,0:T(8,128)(2,1)} %fusion.1.w_ref), custom_call_target="tpu_custom_call" | custom-call | tf_op jit(solution)/shard_map/pallas_call | solution.py:169
  58.2 12.3 %shard_map.47 = bf16[16,2,512,256]{3,2,1,0:T(8,128)(2,1)} custom-call(bf16[128,32,512]{2,1,0:T(8,128)(2,1)} %bitcast.32, bf16[128,32,256]{2,1,0:T(8,128)(2,1)} %bitcast.33), custom_call_target="tpu_custom_call" | custom-call | flops 2147483648 | bytes 14680064 | tf_op jit(solution)/shard_map/pallas_call | solution.py:250
  (7 shorter events, 0.1 us)

commit v11 on v10

--- a/solution.py
+++ b/solution.py
@@ -16,7 +16,7 @@
 floor_level = 0.5
 
 
-def analysis_kernel(fir_taps, bins):
+def analysis_kernel(fir_taps, bins, offset, length):
     span = WL + TAPS - 1
     sample_times = jnp.arange(WL, dtype=jnp.int32)
     phase_index = bins[:, None] * sample_times[None, :] % WL
@@ -27,9 +27,11 @@
         2 * F, WL
     )
     lanes = 128
-    blocks = pl_cdiv(span, lanes)
+    blocks = pl_cdiv(length, lanes)
     width = 2 * lanes
-    padded = jnp.pad(pattern, ((0, 0), (TAPS - 1, blocks * lanes + lanes - WL - (TAPS - 1))))
+    padded = lax.dynamic_update_slice(
+        jnp.zeros((2 * F, (blocks + 1) * lanes), jnp.float32), pattern, (0, TAPS - 1 + offset)
+    )
     windows = jnp.concatenate(
         [
             padded[:, : blocks * lanes].reshape(2 * F, blocks, lanes),
@@ -45,7 +47,7 @@
         band,
         precision=lax.Precision.HIGHEST,
         preferred_element_type=jnp.float32,
-    ).reshape(2 * F, blocks * lanes)[:, :span]
+    ).reshape(2 * F, blocks * lanes)[:, :length]
     return kernel.astype(jnp.bfloat16)
 
 
@@ -182,14 +184,9 @@
 
 
 def on_device(record, fir_taps, bins, offsets):
-    kernel = analysis_kernel(fir_taps, bins)
-    span = WL + TAPS - 1
     local_count = offsets.shape[0]
-
     assert local_count == 1
-    placed = lax.dynamic_update_slice(
-        jnp.zeros((kernel.shape[0], record.shape[0]), kernel.dtype), kernel, (0, offsets[0])
-    )
+    placed = analysis_kernel(fir_taps, bins, offsets[0], record.shape[0])
     spectra = jnp.dot(placed, record, preferred_element_type=jnp.float32)[None]
     whitened = whiten(spectra)
     channels = whitened.shape[-1]

time: 70.7 us -> 70.9 us (level)
  no operation moved by 1% of the time
where the time goes in v11:
time: 70.9 us; the launch traced here: 70.8 us
  Pallas kernels  59.1 us (83%)
  matrix products  6.85 us (10%)
  local copies, waits for them, and re-layouts  2.03 us (3%)
  other arithmetic  2.02 us (3%)
  between operations  0.75 us (1%)
    pallas_call x1, Pallas kernels, exchange(): pl.pallas_call(functools.partial(exchange_kernel, nr, nc), out_shape=(jax...  46.8 us
    pallas_call x1, Pallas kernels, cross(): pl.pallas_call(functools.partial(cross_kernel, scale, chunks), out_shape=...  12.3 us
    dot_general x1, matrix products, on_device(): spectra = jnp.dot(placed, record, preferred_element_type=jnp.float32)[None]  6.39 us

profile of v11, /device:TPU:0, one launch (start us, length us, event | category | flops | bytes accessed | tf_op | source)
XLA Modules:
  0.0 70.8 jit_solution(5356883835075080522)
XLA Ops:
  0.7 0.7 concatenate.7
  1.3 0.1 subtract_multiply_fusion
  1.4 1.1 %cosine_multiply_fusion = (f32[1,16,1280]{2,1,0:T(8,128)S(1)}, f32[1,16,1280]{2,1,0:T(8,128)S(1)}) fusion(f32[1280]{0:T(1024)S(1)} %subtract_multiply_fusion, s32[16]{0:T(128)} %param.6), kind=kLoop, calls=%fused_computation.26 | loop fusion | flops 245760 | bytes 169024 | tf_op jit(solution)/shard_map/mul | solution.py:26
  2.5 0.3 tile.10
  2.9 0.9 %dynamic_update_slice.3 = f32[32,1536]{1,0:T(8,128)S(1)} dynamic-update-slice(f32[32,1536]{1,0:T(8,128)S(1)} %broadcast_in_dim.2, f32[32,1280]{1,0:T(8,128)S(1)} %bitcast.30, s32[]{:T(128)} %constant.14.clone.1, s32[]{:T(128)S(6)} %select_n.22) | dynamic-update-slice | bytes 327684 | tf_op jit(solution)/shard_map/dynamic_update_slice | solution.py:32
  3.9 0.5 fusion
  4.4 6.4 %fusion.10 = f32[32,4096]{1,0:T(8,128)S(1)} fusion(bf16[1408,4096]{1,0:T(8,128)(2,1)} %param.4, bf16[11,4,8,128]{3,2,1,0:T(8,128)(2,1)S(1)} %fusion), kind=kOutput, calls=%fused_computation.20 | convolution fusion | flops 369098752 | bytes 12148736 | tf_op jit(solution)/shard_map/dot_general | solution.py:190
  10.8 0.1 fusion.9
  10.9 0.7 %fusion.1.w_ref = bf16[32,4096]{1,0:T(8,128)(2,1)} fusion(f32[32,4096]{1,0:T(8,128)S(1)} %fusion.10, f32[16,4096]{1,0:T(8,128)S(1)} %fusion.9), kind=kLoop, calls=%fused_computation.3 | loop fusion | flops 262144 | bytes 1048576 | tf_op jit(solution)/shard_map/convert_element_type | solution.py:62
  11.6 46.8 %shard_map.46 = (bf16[16,8,32,512]{3,2,1,0:T(8,128)(2,1)}, bf16[16,8,32,256]{3,2,1,0:T(8,128)(2,1)}) custom-call(bf16[32,4096]{1,0:T(8,128)(2,1)} %fusion.1.w_ref), custom_call_target="tpu_custom_call" | custom-call | tf_op jit(solution)/shard_map/pallas_call | solution.py:171
  58.4 12.3 %shard_map.47 = bf16[16,2,512,256]{3,2,1,0:T(8,128)(2,1)} custom-call(bf16[128,32,512]{2,1,0:T(8,128)(2,1)} %bitcast.28, bf16[128,32,256]{2,1,0:T(8,128)(2,1)} %bitcast.29), custom_call_target="tpu_custom_call" | custom-call | flops 2147483648 | bytes 14680064 | tf_op jit(solution)/shard_map/pallas_call | solution.py:247
  (7 shorter events, 0.1 us)

commit v12 on v10

--- a/solution.py
+++ b/solution.py
@@ -227,7 +227,7 @@
             copies[2 * i].wait()
             lt[:, part, :] = pltpu.einshape("nkc->knc", l_in[part])
             copies[2 * i + 1].wait()
-            rt[:, part, :] = pltpu.einshape("nkc->knc", r_in[part])
+            rt[:, part, :] = pltpu.einshape("nkc->knc", r_in[part]) * jnp.asarray(scale, rt.dtype)
 
     l0, l1 = lt[f], lt[f + bins]
     r0, r1 = rt[f], rt[f + bins]
@@ -238,8 +238,8 @@
     both = lax.dot_general(
         lhs, rhs, (((0,), (0,)), ((), ())), preferred_element_type=jnp.float32
     )
-    out_ref[0, 0] = (both[:, :cb] * scale).astype(out_ref.dtype)
-    out_ref[0, 1] = (both[:, cb:] * scale).astype(out_ref.dtype)
+    out_ref[0, 0] = both[:, :cb].astype(out_ref.dtype)
+    out_ref[0, 1] = both[:, cb:].astype(out_ref.dtype)
 
 
 def cross(left, right, scale):

time: 70.7 us -> 70.7 us (level)
  no operation moved by 1% of the time
where the time goes in v12:
time: 70.7 us; the launch traced here: 70.5 us
  Pallas kernels  58.8 us (83%)
  matrix products  6.82 us (10%)
  local copies, waits for them, and re-layouts  2.06 us (3%)
  other arithmetic  2.02 us (3%)
  between operations  0.76 us (1%)
    pallas_call x1, Pallas kernels, exchange(): pl.pallas_call(functools.partial(exchange_kernel, nr, nc), out_shape=(jax...  46.5 us
    pallas_call x1, Pallas kernels, cross(): pl.pallas_call(functools.partial(cross_kernel, scale, chunks), out_shape=...  12.3 us
    dot_general x1, matrix products, on_device(): spectra = jnp.dot(placed, record, preferred_element_type=jnp.float32)[None]  6.36 us

profile of v12, /device:TPU:0, one launch (start us, length us, event | category | flops | bytes accessed | tf_op | source)
XLA Modules:
  0.0 70.5 jit_solution(18398275451324444273)
XLA Ops:
  0.7 0.7 concatenate.7
  1.3 0.1 subtract_multiply_fusion
  1.4 1.1 %cosine_multiply_fusion = (f32[1,16,1280]{2,1,0:T(8,128)S(1)}, f32[1,16,1280]{2,1,0:T(8,128)S(1)}) fusion(f32[1280]{0:T(1024)S(1)} %subtract_multiply_fusion, s32[16]{0:T(128)} %param.6), kind=kLoop, calls=%fused_computation.26 | loop fusion | flops 245760 | bytes 169024 | tf_op jit(solution)/shard_map/mul | solution.py:26
  2.5 0.3 tile.10
  2.9 0.1 fusion.10
  3.1 0.5 fusion
  3.6 0.8 %dynamic_update_slice.3 = bf16[32,1408]{1,0:T(8,128)(2,1)S(1)} dynamic-update-slice(bf16[32,1408]{1,0:T(8,128)(2,1)S(1)} %broadcast_in_dim.2, bf16[32,1380]{1,0:T(8,128)(2,1)S(1)} %bitcast.35, s32[]{:T(128)} %constant.12.clone.1, s32[]{:T(128)S(6)} %select_n.22) | dynamic-update-slice | bytes 176644 | tf_op jit(solution)/shard_map/dynamic_update_slice | solution.py:190
  4.4 6.4 %fusion.18 = f32[32,4096]{1,0:T(8,128)S(1)} fusion(bf16[32,1408]{1,0:T(8,128)(2,1)S(1)} %dynamic_update_slice.3, bf16[1408,4096]{1,0:T(8,128)(2,1)} %param.4), kind=kOutput, calls=%fused_computation.33 | convolution fusion | flops 369098752 | bytes 12148736 | tf_op jit(solution)/shard_map/dot_general | solution.py:193
  10.8 0.1 fusion.9
  10.9 0.7 %fusion.1.w_ref = bf16[32,4096]{1,0:T(8,128)(2,1)} fusion(f32[32,4096]{1,0:T(8,128)S(1)} %fusion.18, f32[16,4096]{1,0:T(8,128)S(1)} %fusion.9), kind=kLoop, calls=%fused_computation.3 | loop fusion | flops 262144 | bytes 1048576 | tf_op jit(solution)/shard_map/convert_element_type | solution.py:60
  11.7 46.5 %shard_map.46 = (bf16[16,8,32,512]{3,2,1,0:T(8,128)(2,1)}, bf16[16,8,32,256]{3,2,1,0:T(8,128)(2,1)}) custom-call(bf16[32,4096]{1,0:T(8,128)(2,1)} %fusion.1.w_ref), custom_call_target="tpu_custom_call" | custom-call | tf_op jit(solution)/shard_map/pallas_call | solution.py:169
  58.2 12.3 %shard_map.47 = bf16[16,2,512,256]{3,2,1,0:T(8,128)(2,1)} custom-call(bf16[128,32,512]{2,1,0:T(8,128)(2,1)} %bitcast.32, bf16[128,32,256]{2,1,0:T(8,128)(2,1)} %bitcast.33), custom_call_target="tpu_custom_call" | custom-call | flops 2147483648 | bytes 14680064 | tf_op jit(solution)/shard_map/pallas_call | solution.py:250
  (7 shorter events, 0.1 us)

commit v13 on v12

--- a/solution.py
+++ b/solution.py
@@ -225,19 +225,17 @@
         for i in range(chunks):
             part = pl.ds(i * size, size)
             copies[2 * i].wait()
-            lt[:, part, :] = pltpu.einshape("nkc->knc", l_in[part])
+            lt[:, :, part] = pltpu.einshape("nkc->kcn", l_in[part])
             copies[2 * i + 1].wait()
             rt[:, part, :] = pltpu.einshape("nkc->knc", r_in[part]) * jnp.asarray(scale, rt.dtype)
 
     l0, l1 = lt[f], lt[f + bins]
     r0, r1 = rt[f], rt[f + bins]
-    lhs = jnp.concatenate([l0, l1], axis=0)
+    lhs = jnp.concatenate([l0, l1], axis=1)
     rhs = jnp.concatenate(
         [jnp.concatenate([r0, r1], axis=1), jnp.concatenate([r1, -r0], axis=1)], axis=0
     )
-    both = lax.dot_general(
-        lhs, rhs, (((0,), (0,)), ((), ())), preferred_element_type=jnp.float32
-    )
+    both = jnp.dot(lhs, rhs, preferred_element_type=jnp.float32)
     out_ref[0, 0] = both[:, :cb].astype(out_ref.dtype)
     out_ref[0, 1] = both[:, cb:].astype(out_ref.dtype)
 
@@ -256,7 +254,7 @@
         scratch_shapes=[
             pltpu.VMEM((windows, parts, rb), left.dtype),
             pltpu.VMEM((windows, parts, cb), right.dtype),
-            pltpu.VMEM((parts, windows, rb), left.dtype),
+            pltpu.VMEM((parts, rb, windows), left.dtype),
             pltpu.VMEM((parts, windows, cb), right.dtype),
             pltpu.SemaphoreType.DMA((2, chunks)),
         ],

time: 70.7 us -> 94.1 us (1.33)
  Pallas kernels: 58.8 us -> 82.1 us
    pallas_call x1, Pallas kernels: 12.3 us -> 35.6 us  [cross(): pl.pallas_call(functools.partial(cross_kernel, scale, chunks), out_shape=...]
where the time goes in v13:
time: 94.1 us; the launch traced here: 93.9 us
  Pallas kernels  82.1 us (87%)
  matrix products  6.82 us (7%)
  local copies, waits for them, and re-layouts  2.06 us (2%)
  other arithmetic  2.02 us (2%)
    pallas_call x1, Pallas kernels, exchange(): pl.pallas_call(functools.partial(exchange_kernel, nr, nc), out_shape=(jax...  46.5 us
    pallas_call x1, Pallas kernels, cross(): pl.pallas_call(functools.partial(cross_kernel, scale, chunks), out_shape=...  35.6 us
    dot_general x1, matrix products, on_device(): spectra = jnp.dot(placed, record, preferred_element_type=jnp.float32)[None]  6.36 us

profile of v13, /device:TPU:0, one launch (start us, length us, event | category | flops | bytes accessed | tf_op | source)
XLA Modules:
  0.0 93.9 jit_solution(7871234449223538200)
XLA Ops:
  0.7 0.7 concatenate.7
  1.3 0.1 subtract_multiply_fusion
  1.4 1.1 %cosine_multiply_fusion = (f32[1,16,1280]{2,1,0:T(8,128)S(1)}, f32[1,16,1280]{2,1,0:T(8,128)S(1)}) fusion(f32[1280]{0:T(1024)S(1)} %subtract_multiply_fusion, s32[16]{0:T(128)} %param.6), kind=kLoop, calls=%fused_computation.26 | loop fusion | flops 245760 | bytes 169024 | tf_op jit(solution)/shard_map/mul | solution.py:26
  2.5 0.3 tile.10
  2.9 0.1 fusion.10
  3.1 0.5 fusion
  3.6 0.8 dynamic_update_slice.3
  4.4 6.4 %fusion.18 = f32[32,4096]{1,0:T(8,128)S(1)} fusion(bf16[32,1408]{1,0:T(8,128)(2,1)S(1)} %dynamic_update_slice.3, bf16[1408,4096]{1,0:T(8,128)(2,1)} %param.4), kind=kOutput, calls=%fused_computation.33 | convolution fusion | flops 369098752 | bytes 12148736 | tf_op jit(solution)/shard_map/dot_general | solution.py:193
  10.8 0.1 fusion.9
  10.9 0.7 fusion.1.w_ref
  11.6 46.5 %shard_map.46 = (bf16[16,8,32,512]{3,2,1,0:T(8,128)(2,1)}, bf16[16,8,32,256]{3,2,1,0:T(8,128)(2,1)}) custom-call(bf16[32,4096]{1,0:T(8,128)(2,1)} %fusion.1.w_ref), custom_call_target="tpu_custom_call" | custom-call | tf_op jit(solution)/shard_map/pallas_call | solution.py:169
  58.2 35.6 %shard_map.47 = bf16[16,2,512,256]{3,2,1,0:T(8,128)(2,1)} custom-call(bf16[128,32,512]{2,1,0:T(8,128)(2,1)} %bitcast.32, bf16[128,32,256]{2,1,0:T(8,128)(2,1)} %bitcast.33), custom_call_target="tpu_custom_call" | custom-call | flops 2147483648 | bytes 14680064 | tf_op jit(solution)/shard_map/pallas_call | solution.py:248
  (7 shorter events, 0.1 us)

commit v14 on v12

--- a/solution.py
+++ b/solution.py
@@ -58,6 +58,34 @@
     magnitude = jnp.sqrt(shaped[:, 0] * shaped[:, 0] + shaped[:, 1] * shaped[:, 1])
     inverse = 1.0 / jnp.maximum(magnitude, floor_level)
     return (shaped * inverse[:, None]).astype(jnp.bfloat16)
+
+
+def spectra_kernel(k_ref, rec_ref, out_ref):
+    spectra = jnp.dot(k_ref[...], rec_ref[...], preferred_element_type=jnp.float32)
+    re, im = spectra[:F], spectra[F:]
+    inverse = 1.0 / jnp.maximum(jnp.sqrt(re * re + im * im), floor_level)
+    out_ref[...] = (spectra * jnp.concatenate([inverse, inverse], axis=0)).astype(out_ref.dtype)
+
+
+def spectra_whitened(placed, record):
+    rows, length = placed.shape
+    channels = record.shape[-1]
+    block = 512
+    return pl.pallas_call(
+        spectra_kernel,
+        out_shape=jax.ShapeDtypeStruct((rows, channels), jnp.bfloat16),
+        grid=(channels // block,),
+        in_specs=[
+            pl.BlockSpec((rows, length), lambda j: (0, 0)),
+            pl.BlockSpec((length, block), lambda j: (0, j)),
+        ],
+        out_specs=pl.BlockSpec((rows, block), lambda j: (0, j)),
+        cost_estimate=pl.CostEstimate(
+            flops=2 * rows * length * channels,
+            bytes_accessed=2 * (placed.size + record.size + rows * channels),
+            transcendentals=2 * F * channels,
+        ),
+    )(placed, record)
 
 
 MESH = pl.DeviceIdType.MESH
@@ -190,8 +218,7 @@
     placed = lax.dynamic_update_slice(
         jnp.zeros((kernel.shape[0], record.shape[0]), kernel.dtype), kernel, (0, offsets[0])
     )
-    spectra = jnp.dot(placed, record, preferred_element_type=jnp.float32)[None]
-    whitened = whiten(spectra)
+    whitened = spectra_whitened(placed, record)[None]
     channels = whitened.shape[-1]
     row_count = lax.axis_size("row")
     col_count = lax.axis_size("col")

time: 70.7 us -> 72.8 us (1.030)
  Pallas kernels: 58.8 us -> 67.4 us
  matrix products: 6.82 us -> 0.46 us
  other arithmetic: 2.02 us -> 1.15 us
    pallas_call x0 -> x1, Pallas kernels: none -> 8.56 us  [spectra_whitened(): pl.pallas_call(spectra_kernel, out_shape=jax.ShapeDtypeStruct((rows, chan...]
    dot_general x1 -> x0, matrix products: 6.36 us -> none  [on_device(): spectra = jnp.dot(placed, record, preferred_element_type=jnp.float32)[None]]
    convert_element_type x1 -> x0, other arithmetic: 0.74 us -> none  [whiten(): return (shaped * inverse[:, None]).astype(jnp.bfloat16)]
where the time goes in v14:
time: 72.8 us; the launch traced here: 72.5 us
  Pallas kernels  67.4 us (93%)
  local copies, waits for them, and re-layouts  2.69 us (4%)
  other arithmetic  1.15 us (2%)
  between operations  0.76 us (1%)
    pallas_call x1, Pallas kernels, exchange(): pl.pallas_call(functools.partial(exchange_kernel, nr, nc), out_shape=(jax...  46.5 us
    pallas_call x1, Pallas kernels, cross(): pl.pallas_call(functools.partial(cross_kernel, scale, chunks), out_shape=...  12.3 us
    pallas_call x1, Pallas kernels, spectra_whitened(): pl.pallas_call(spectra_kernel, out_shape=jax.ShapeDtypeStruct((rows, chan...  8.56 us

profile of v14, /device:TPU:0, one launch (start us, length us, event | category | flops | bytes accessed | tf_op | source)
XLA Modules:
  0.0 72.5 jit_solution(1435867883430813630)
XLA Ops:
  0.7 0.7 concatenate.7
  1.3 0.1 subtract_multiply_fusion
  1.4 1.1 %cosine_multiply_fusion = (f32[1,16,1280]{2,1,0:T(8,128)S(1)}, f32[1,16,1280]{2,1,0:T(8,128)S(1)}) fusion(f32[1280]{0:T(1024)S(1)} %subtract_multiply_fusion, s32[16]{0:T(128)} %param.6), kind=kLoop, calls=%fused_computation.17 | loop fusion | flops 245760 | bytes 169024 | tf_op jit(solution)/shard_map/mul | solution.py:26
  2.5 0.3 tile.10
  2.9 0.1 fusion.4
  3.1 0.5 fusion
  3.6 0.8 %dynamic_update_slice.3.k_ref = bf16[32,1408]{1,0:T(8,128)(2,1)S(1)} dynamic-update-slice(bf16[32,1408]{1,0:T(8,128)(2,1)S(1)} %broadcast_in_dim.2, bf16[32,1380]{1,0:T(8,128)(2,1)S(1)} %bitcast.25, s32[]{:T(128)} %constant.12.clone.1, s32[]{:T(128)S(6)} %select_n.22) | dynamic-update-slice | bytes 176644 | tf_op jit(solution)/shard_map/dynamic_update_slice | solution.py:218
  4.4 0.0 copy-start
  4.4 0.6 copy-done
  5.1 8.6 %shard_map.46.w_ref = bf16[32,4096]{1,0:T(8,128)(2,1)} custom-call(bf16[32,1408]{1,0:T(8,128)(2,1)} %copy-done, bf16[1408,4096]{1,0:T(8,128)(2,1)} %rec_ref.1), custom_call_target="tpu_custom_call" | custom-call | flops 369098752 | bytes 11886592 | tf_op jit(solution)/shard_map/pallas_call | solution.py:74
  13.6 46.5 %shard_map.47 = (bf16[16,8,32,512]{3,2,1,0:T(8,128)(2,1)}, bf16[16,8,32,256]{3,2,1,0:T(8,128)(2,1)}) custom-call(bf16[32,4096]{1,0:T(8,128)(2,1)} %shard_map.46.w_ref), custom_call_target="tpu_custom_call" | custom-call | tf_op jit(solution)/shard_map/pallas_call | solution.py:197
  60.1 12.3 %shard_map.48 = bf16[16,2,512,256]{3,2,1,0:T(8,128)(2,1)} custom-call(bf16[128,32,512]{2,1,0:T(8,128)(2,1)} %bitcast.22, bf16[128,32,256]{2,1,0:T(8,128)(2,1)} %bitcast.23), custom_call_target="tpu_custom_call" | custom-call | flops 2147483648 | bytes 14680064 | tf_op jit(solution)/shard_map/pallas_call | solution.py:277
  (7 shorter events, 0.1 us)
Async XLA Ops:
  4.4 0.6 copy-start

commit v15 on v12

--- a/solution.py
+++ b/solution.py
@@ -246,7 +246,7 @@
     windows, parts, rb = left.shape
     cb = right.shape[-1]
     bins = parts // 2
-    chunks = 8
+    chunks = 16
     return pl.pallas_call(
         functools.partial(cross_kernel, scale, chunks),
         out_shape=jax.ShapeDtypeStruct((bins, 2, rb, cb), jnp.bfloat16),

time: 70.7 us -> 70.8 us (level)
  no operation moved by 1% of the time
where the time goes in v15:
time: 70.8 us; the launch traced here: 70.6 us
  Pallas kernels  58.9 us (83%)
  matrix products  6.82 us (10%)
  local copies, waits for them, and re-layouts  2.06 us (3%)
  other arithmetic  2.02 us (3%)
  between operations  0.76 us (1%)
    pallas_call x1, Pallas kernels, exchange(): pl.pallas_call(functools.partial(exchange_kernel, nr, nc), out_shape=(jax...  46.5 us
    pallas_call x1, Pallas kernels, cross(): pl.pallas_call(functools.partial(cross_kernel, scale, chunks), out_shape=...  12.4 us
    dot_general x1, matrix products, on_device(): spectra = jnp.dot(placed, record, preferred_element_type=jnp.float32)[None]  6.36 us

profile of v15, /device:TPU:0, one launch (start us, length us, event | category | flops | bytes accessed | tf_op | source)
XLA Modules:
  0.0 70.6 jit_solution(18439497073025042321)
XLA Ops:
  0.7 0.7 concatenate.7
  1.3 0.1 subtract_multiply_fusion
  1.4 1.1 %cosine_multiply_fusion = (f32[1,16,1280]{2,1,0:T(8,128)S(1)}, f32[1,16,1280]{2,1,0:T(8,128)S(1)}) fusion(f32[1280]{0:T(1024)S(1)} %subtract_multiply_fusion, s32[16]{0:T(128)} %param.6), kind=kLoop, calls=%fused_computation.26 | loop fusion | flops 245760 | bytes 169024 | tf_op jit(solution)/shard_map/mul | solution.py:26
  2.5 0.3 tile.10
  2.9 0.1 fusion.10
  3.1 0.5 fusion
  3.6 0.8 %dynamic_update_slice.3 = bf16[32,1408]{1,0:T(8,128)(2,1)S(1)} dynamic-update-slice(bf16[32,1408]{1,0:T(8,128)(2,1)S(1)} %broadcast_in_dim.2, bf16[32,1380]{1,0:T(8,128)(2,1)S(1)} %bitcast.35, s32[]{:T(128)} %constant.12.clone.1, s32[]{:T(128)S(6)} %select_n.22) | dynamic-update-slice | bytes 176644 | tf_op jit(solution)/shard_map/dynamic_update_slice | solution.py:190
  4.4 6.4 %fusion.18 = f32[32,4096]{1,0:T(8,128)S(1)} fusion(bf16[32,1408]{1,0:T(8,128)(2,1)S(1)} %dynamic_update_slice.3, bf16[1408,4096]{1,0:T(8,128)(2,1)} %param.4), kind=kOutput, calls=%fused_computation.33 | convolution fusion | flops 369098752 | bytes 12148736 | tf_op jit(solution)/shard_map/dot_general | solution.py:193
  10.8 0.1 fusion.9
  10.9 0.7 %fusion.1.w_ref = bf16[32,4096]{1,0:T(8,128)(2,1)} fusion(f32[32,4096]{1,0:T(8,128)S(1)} %fusion.18, f32[16,4096]{1,0:T(8,128)S(1)} %fusion.9), kind=kLoop, calls=%fused_computation.3 | loop fusion | flops 262144 | bytes 1048576 | tf_op jit(solution)/shard_map/convert_element_type | solution.py:60
  11.7 46.5 %shard_map.46 = (bf16[16,8,32,512]{3,2,1,0:T(8,128)(2,1)}, bf16[16,8,32,256]{3,2,1,0:T(8,128)(2,1)}) custom-call(bf16[32,4096]{1,0:T(8,128)(2,1)} %fusion.1.w_ref), custom_call_target="tpu_custom_call" | custom-call | tf_op jit(solution)/shard_map/pallas_call | solution.py:169
  58.2 12.4 %shard_map.47 = bf16[16,2,512,256]{3,2,1,0:T(8,128)(2,1)} custom-call(bf16[128,32,512]{2,1,0:T(8,128)(2,1)} %bitcast.32, bf16[128,32,256]{2,1,0:T(8,128)(2,1)} %bitcast.33), custom_call_target="tpu_custom_call" | custom-call | flops 2147483648 | bytes 14680064 | tf_op jit(solution)/shard_map/pallas_call | solution.py:250
  (7 shorter events, 0.1 us)

commit v16 on v15

--- a/solution.py
+++ b/solution.py
@@ -209,7 +209,6 @@
 
 def cross_kernel(scale, chunks, l_hbm, r_hbm, out_ref, l_in, r_in, lt, rt, sems):
     f = pl.program_id(0)
-    bins = pl.num_programs(0)
     cb = r_hbm.shape[-1]
     size = l_hbm.shape[0] // chunks
 
@@ -229,17 +228,21 @@
             copies[2 * i + 1].wait()
             rt[:, part, :] = pltpu.einshape("nkc->knc", r_in[part]) * jnp.asarray(scale, rt.dtype)
 
-    l0, l1 = lt[f], lt[f + bins]
-    r0, r1 = rt[f], rt[f + bins]
-    lhs = jnp.concatenate([l0, l1], axis=0)
-    rhs = jnp.concatenate(
-        [jnp.concatenate([r0, r1], axis=1), jnp.concatenate([r1, -r0], axis=1)], axis=0
-    )
-    both = lax.dot_general(
-        lhs, rhs, (((0,), (0,)), ((), ())), preferred_element_type=jnp.float32
-    )
-    out_ref[0, 0] = both[:, :cb].astype(out_ref.dtype)
-    out_ref[0, 1] = both[:, cb:].astype(out_ref.dtype)
+    per_step = out_ref.shape[0]
+    half = lt.shape[0] // 2
+    for t in range(per_step):
+        b = f * per_step + t
+        l0, l1 = lt[b], lt[b + half]
+        r0, r1 = rt[b], rt[b + half]
+        lhs = jnp.concatenate([l0, l1], axis=0)
+        rhs = jnp.concatenate(
+            [jnp.concatenate([r0, r1], axis=1), jnp.concatenate([r1, -r0], axis=1)], axis=0
+        )
+        both = lax.dot_general(
+            lhs, rhs, (((0,), (0,)), ((), ())), preferred_element_type=jnp.float32
+        )
+        out_ref[t, 0] = both[:, :cb].astype(out_ref.dtype)
+        out_ref[t, 1] = both[:, cb:].astype(out_ref.dtype)
 
 
 def cross(left, right, scale):
@@ -247,12 +250,13 @@
     cb = right.shape[-1]
     bins = parts // 2
     chunks = 16
+    per_step = 2
     return pl.pallas_call(
         functools.partial(cross_kernel, scale, chunks),
         out_shape=jax.ShapeDtypeStruct((bins, 2, rb, cb), jnp.bfloat16),
-        grid=(bins,),
+        grid=(bins // per_step,),
         in_specs=[pl.BlockSpec(memory_space=pl.ANY), pl.BlockSpec(memory_space=pl.ANY)],
-        out_specs=pl.BlockSpec((1, 2, rb, cb), lambda f: (f, 0, 0, 0)),
+        out_specs=pl.BlockSpec((per_step, 2, rb, cb), lambda f: (f, 0, 0, 0)),
         scratch_shapes=[
             pltpu.VMEM((windows, parts, rb), left.dtype),
             pltpu.VMEM((windows, parts, cb), right.dtype),

time: 70.8 us -> 67.7 us (0.956)
  Pallas kernels: 58.9 us -> 55.9 us
    pallas_call x1, Pallas kernels: 12.4 us -> 9.36 us  [cross(): pl.pallas_call(functools.partial(cross_kernel, scale, chunks), out_shape=...]
where the time goes in v16:
time: 67.7 us; the launch traced here: 67.5 us
  Pallas kernels  55.9 us (83%)
  matrix products  6.82 us (10%)
  local copies, waits for them, and re-layouts  2.06 us (3%)
  other arithmetic  2.02 us (3%)
  between operations  0.76 us (1%)
    pallas_call x1, Pallas kernels, exchange(): pl.pallas_call(functools.partial(exchange_kernel, nr, nc), out_shape=(jax...  46.5 us
    pallas_call x1, Pallas kernels, cross(): pl.pallas_call(functools.partial(cross_kernel, scale, chunks), out_shape=...  9.36 us
    dot_general x1, matrix products, on_device(): spectra = jnp.dot(placed, record, preferred_element_type=jnp.float32)[None]  6.36 us

profile of v16, /device:TPU:0, one launch (start us, length us, event | category | flops | bytes accessed | tf_op | source)
XLA Modules:
  0.0 67.5 jit_solution(17985765411954567324)
XLA Ops:
  0.7 0.7 concatenate.7
  1.3 0.1 subtract_multiply_fusion
  1.4 1.1 %cosine_multiply_fusion = (f32[1,16,1280]{2,1,0:T(8,128)S(1)}, f32[1,16,1280]{2,1,0:T(8,128)S(1)}) fusion(f32[1280]{0:T(1024)S(1)} %subtract_multiply_fusion, s32[16]{0:T(128)} %param.6), kind=kLoop, calls=%fused_computation.26 | loop fusion | flops 245760 | bytes 169024 | tf_op jit(solution)/shard_map/mul | solution.py:26
  2.5 0.3 tile.10
  2.9 0.1 fusion.10
  3.1 0.5 fusion
  3.6 0.8 %dynamic_update_slice.3 = bf16[32,1408]{1,0:T(8,128)(2,1)S(1)} dynamic-update-slice(bf16[32,1408]{1,0:T(8,128)(2,1)S(1)} %broadcast_in_dim.2, bf16[32,1380]{1,0:T(8,128)(2,1)S(1)} %bitcast.35, s32[]{:T(128)} %constant.12.clone.1, s32[]{:T(128)S(6)} %select_n.22) | dynamic-update-slice | bytes 176644 | tf_op jit(solution)/shard_map/dynamic_update_slice | solution.py:190
  4.4 6.4 %fusion.18 = f32[32,4096]{1,0:T(8,128)S(1)} fusion(bf16[32,1408]{1,0:T(8,128)(2,1)S(1)} %dynamic_update_slice.3, bf16[1408,4096]{1,0:T(8,128)(2,1)} %param.4), kind=kOutput, calls=%fused_computation.33 | convolution fusion | flops 369098752 | bytes 12148736 | tf_op jit(solution)/shard_map/dot_general | solution.py:193
  10.8 0.1 fusion.9
  10.9 0.7 %fusion.1.w_ref = bf16[32,4096]{1,0:T(8,128)(2,1)} fusion(f32[32,4096]{1,0:T(8,128)S(1)} %fusion.18, f32[16,4096]{1,0:T(8,128)S(1)} %fusion.9), kind=kLoop, calls=%fused_computation.3 | loop fusion | flops 262144 | bytes 1048576 | tf_op jit(solution)/shard_map/convert_element_type | solution.py:60
  11.7 46.5 %shard_map.46 = (bf16[16,8,32,512]{3,2,1,0:T(8,128)(2,1)}, bf16[16,8,32,256]{3,2,1,0:T(8,128)(2,1)}) custom-call(bf16[32,4096]{1,0:T(8,128)(2,1)} %fusion.1.w_ref), custom_call_target="tpu_custom_call" | custom-call | tf_op jit(solution)/shard_map/pallas_call | solution.py:169
  58.2 9.4 %shard_map.47 = bf16[16,2,512,256]{3,2,1,0:T(8,128)(2,1)} custom-call(bf16[128,32,512]{2,1,0:T(8,128)(2,1)} %bitcast.32, bf16[128,32,256]{2,1,0:T(8,128)(2,1)} %bitcast.33), custom_call_target="tpu_custom_call" | custom-call | flops 2147483648 | bytes 14680064 | tf_op jit(solution)/shard_map/pallas_call | solution.py:254
  (7 shorter events, 0.1 us)

commit v17 on v16

--- a/solution.py
+++ b/solution.py
@@ -250,7 +250,7 @@
     cb = right.shape[-1]
     bins = parts // 2
     chunks = 16
-    per_step = 2
+    per_step = 4
     return pl.pallas_call(
         functools.partial(cross_kernel, scale, chunks),
         out_shape=jax.ShapeDtypeStruct((bins, 2, rb, cb), jnp.bfloat16),

time: 67.7 us -> 66.4 us (0.981)
  Pallas kernels: 55.9 us -> 54.5 us
    pallas_call x1, Pallas kernels: 9.36 us -> 8.01 us  [cross(): pl.pallas_call(functools.partial(cross_kernel, scale, chunks), out_shape=...]
where the time goes in v17:
time: 66.4 us; the launch traced here: 66.2 us
  Pallas kernels  54.5 us (82%)
  matrix products  6.82 us (10%)
  local copies, waits for them, and re-layouts  2.06 us (3%)
  other arithmetic  2.02 us (3%)
  between operations  0.76 us (1%)
    pallas_call x1, Pallas kernels, exchange(): pl.pallas_call(functools.partial(exchange_kernel, nr, nc), out_shape=(jax...  46.5 us
    pallas_call x1, Pallas kernels, cross(): pl.pallas_call(functools.partial(cross_kernel, scale, chunks), out_shape=...  8.01 us
    dot_general x1, matrix products, on_device(): spectra = jnp.dot(placed, record, preferred_element_type=jnp.float32)[None]  6.36 us

profile of v17, /device:TPU:0, one launch (start us, length us, event | category | flops | bytes accessed | tf_op | source)
XLA Modules:
  0.0 66.2 jit_solution(11586530375722688673)
XLA Ops:
  0.7 0.7 concatenate.7
  1.3 0.1 subtract_multiply_fusion
  1.4 1.1 %cosine_multiply_fusion = (f32[1,16,1280]{2,1,0:T(8,128)S(1)}, f32[1,16,1280]{2,1,0:T(8,128)S(1)}) fusion(f32[1280]{0:T(1024)S(1)} %subtract_multiply_fusion, s32[16]{0:T(128)} %param.6), kind=kLoop, calls=%fused_computation.26 | loop fusion | flops 245760 | bytes 169024 | tf_op jit(solution)/shard_map/mul | solution.py:26
  2.5 0.3 tile.10
  2.9 0.1 fusion.10
  3.1 0.5 fusion
  3.6 0.8 %dynamic_update_slice.3 = bf16[32,1408]{1,0:T(8,128)(2,1)S(1)} dynamic-update-slice(bf16[32,1408]{1,0:T(8,128)(2,1)S(1)} %broadcast_in_dim.2, bf16[32,1380]{1,0:T(8,128)(2,1)S(1)} %bitcast.35, s32[]{:T(128)} %constant.12.clone.1, s32[]{:T(128)S(6)} %select_n.22) | dynamic-update-slice | bytes 176644 | tf_op jit(solution)/shard_map/dynamic_update_slice | solution.py:190
  4.4 6.4 %fusion.18 = f32[32,4096]{1,0:T(8,128)S(1)} fusion(bf16[32,1408]{1,0:T(8,128)(2,1)S(1)} %dynamic_update_slice.3, bf16[1408,4096]{1,0:T(8,128)(2,1)} %param.4), kind=kOutput, calls=%fused_computation.33 | convolution fusion | flops 369098752 | bytes 12148736 | tf_op jit(solution)/shard_map/dot_general | solution.py:193
  10.8 0.1 fusion.9
  10.9 0.7 %fusion.1.w_ref = bf16[32,4096]{1,0:T(8,128)(2,1)} fusion(f32[32,4096]{1,0:T(8,128)S(1)} %fusion.18, f32[16,4096]{1,0:T(8,128)S(1)} %fusion.9), kind=kLoop, calls=%fused_computation.3 | loop fusion | flops 262144 | bytes 1048576 | tf_op jit(solution)/shard_map/convert_element_type | solution.py:60
  11.7 46.5 %shard_map.46 = (bf16[16,8,32,512]{3,2,1,0:T(8,128)(2,1)}, bf16[16,8,32,256]{3,2,1,0:T(8,128)(2,1)}) custom-call(bf16[32,4096]{1,0:T(8,128)(2,1)} %fusion.1.w_ref), custom_call_target="tpu_custom_call" | custom-call | tf_op jit(solution)/shard_map/pallas_call | solution.py:169
  58.2 8.0 %shard_map.47 = bf16[16,2,512,256]{3,2,1,0:T(8,128)(2,1)} custom-call(bf16[128,32,512]{2,1,0:T(8,128)(2,1)} %bitcast.32, bf16[128,32,256]{2,1,0:T(8,128)(2,1)} %bitcast.33), custom_call_target="tpu_custom_call" | custom-call | flops 2147483648 | bytes 14680064 | tf_op jit(solution)/shard_map/pallas_call | solution.py:254
  (7 shorter events, 0.1 us)

commit v18 on v17

--- a/solution.py
+++ b/solution.py
@@ -250,7 +250,7 @@
     cb = right.shape[-1]
     bins = parts // 2
     chunks = 16
-    per_step = 4
+    per_step = 8
     return pl.pallas_call(
         functools.partial(cross_kernel, scale, chunks),
         out_shape=jax.ShapeDtypeStruct((bins, 2, rb, cb), jnp.bfloat16),

time: 66.4 us -> 66.2 us (level)
  no operation moved by 1% of the time
where the time goes in v18:
time: 66.2 us; the launch traced here: 66 us
  Pallas kernels  54.3 us (82%)
  matrix products  6.82 us (10%)
  local copies, waits for them, and re-layouts  2.06 us (3%)
  other arithmetic  2.02 us (3%)
  between operations  0.76 us (1%)
    pallas_call x1, Pallas kernels, exchange(): pl.pallas_call(functools.partial(exchange_kernel, nr, nc), out_shape=(jax...  46.5 us
    pallas_call x1, Pallas kernels, cross(): pl.pallas_call(functools.partial(cross_kernel, scale, chunks), out_shape=...  7.82 us
    dot_general x1, matrix products, on_device(): spectra = jnp.dot(placed, record, preferred_element_type=jnp.float32)[None]  6.36 us

profile of v18, /device:TPU:0, one launch (start us, length us, event | category | flops | bytes accessed | tf_op | source)
XLA Modules:
  0.0 66.0 jit_solution(2276869791416005374)
XLA Ops:
  0.7 0.7 concatenate.7
  1.3 0.1 subtract_multiply_fusion
  1.4 1.1 %cosine_multiply_fusion = (f32[1,16,1280]{2,1,0:T(8,128)S(1)}, f32[1,16,1280]{2,1,0:T(8,128)S(1)}) fusion(f32[1280]{0:T(1024)S(1)} %subtract_multiply_fusion, s32[16]{0:T(128)} %param.6), kind=kLoop, calls=%fused_computation.26 | loop fusion | flops 245760 | bytes 169024 | tf_op jit(solution)/shard_map/mul | solution.py:26
  2.5 0.3 tile.10
  2.9 0.1 fusion.10
  3.1 0.5 fusion
  3.6 0.8 %dynamic_update_slice.3 = bf16[32,1408]{1,0:T(8,128)(2,1)S(1)} dynamic-update-slice(bf16[32,1408]{1,0:T(8,128)(2,1)S(1)} %broadcast_in_dim.2, bf16[32,1380]{1,0:T(8,128)(2,1)S(1)} %bitcast.35, s32[]{:T(128)} %constant.12.clone.1, s32[]{:T(128)S(6)} %select_n.22) | dynamic-update-slice | bytes 176644 | tf_op jit(solution)/shard_map/dynamic_update_slice | solution.py:190
  4.4 6.4 %fusion.18 = f32[32,4096]{1,0:T(8,128)S(1)} fusion(bf16[32,1408]{1,0:T(8,128)(2,1)S(1)} %dynamic_update_slice.3, bf16[1408,4096]{1,0:T(8,128)(2,1)} %param.4), kind=kOutput, calls=%fused_computation.33 | convolution fusion | flops 369098752 | bytes 12148736 | tf_op jit(solution)/shard_map/dot_general | solution.py:193
  10.8 0.1 fusion.9
  10.9 0.7 %fusion.1.w_ref = bf16[32,4096]{1,0:T(8,128)(2,1)} fusion(f32[32,4096]{1,0:T(8,128)S(1)} %fusion.18, f32[16,4096]{1,0:T(8,128)S(1)} %fusion.9), kind=kLoop, calls=%fused_computation.3 | loop fusion | flops 262144 | bytes 1048576 | tf_op jit(solution)/shard_map/convert_element_type | solution.py:60
  11.7 46.5 %shard_map.46 = (bf16[16,8,32,512]{3,2,1,0:T(8,128)(2,1)}, bf16[16,8,32,256]{3,2,1,0:T(8,128)(2,1)}) custom-call(bf16[32,4096]{1,0:T(8,128)(2,1)} %fusion.1.w_ref), custom_call_target="tpu_custom_call" | custom-call | tf_op jit(solution)/shard_map/pallas_call | solution.py:169
  58.2 7.8 %shard_map.47 = bf16[16,2,512,256]{3,2,1,0:T(8,128)(2,1)} custom-call(bf16[128,32,512]{2,1,0:T(8,128)(2,1)} %bitcast.32, bf16[128,32,256]{2,1,0:T(8,128)(2,1)} %bitcast.33), custom_call_target="tpu_custom_call" | custom-call | flops 2147483648 | bytes 14680064 | tf_op jit(solution)/shard_map/pallas_call | solution.py:254
  (7 shorter events, 0.1 us)

commit v19 on v18

--- a/solution.py
+++ b/solution.py
@@ -207,31 +207,26 @@
     return cross(left, right, 1.0 / total_windows)
 
 
-def cross_kernel(scale, chunks, l_hbm, r_hbm, out_ref, l_in, r_in, lt, rt, sems):
-    f = pl.program_id(0)
+def cross_kernel(scale, chunks, l_hbm, r_hbm, out_hbm, l_in, r_in, lt, rt, out_v, sems, out_sems):
     cb = r_hbm.shape[-1]
     size = l_hbm.shape[0] // chunks
-
-    @pl.when(f == 0)
-    def _():
-        copies = []
-        for i in range(chunks):
-            part = pl.ds(i * size, size)
-            for j, (src, dst) in enumerate(((l_hbm, l_in), (r_hbm, r_in))):
-                cp = pltpu.make_async_copy(src.at[part], dst.at[part], sems.at[j, i])
-                cp.start()
-                copies.append(cp)
-        for i in range(chunks):
-            part = pl.ds(i * size, size)
-            copies[2 * i].wait()
-            lt[:, part, :] = pltpu.einshape("nkc->knc", l_in[part])
-            copies[2 * i + 1].wait()
-            rt[:, part, :] = pltpu.einshape("nkc->knc", r_in[part]) * jnp.asarray(scale, rt.dtype)
-
-    per_step = out_ref.shape[0]
+    copies = []
+    for i in range(chunks):
+        part = pl.ds(i * size, size)
+        for j, (src, dst) in enumerate(((l_hbm, l_in), (r_hbm, r_in))):
+            cp = pltpu.make_async_copy(src.at[part], dst.at[part], sems.at[j, i])
+            cp.start()
+            copies.append(cp)
+    for i in range(chunks):
+        part = pl.ds(i * size, size)
+        copies[2 * i].wait()
+        lt[:, part, :] = pltpu.einshape("nkc->knc", l_in[part])
+        copies[2 * i + 1].wait()
+        rt[:, part, :] = pltpu.einshape("nkc->knc", r_in[part]) * jnp.asarray(scale, rt.dtype)
+
     half = lt.shape[0] // 2
-    for t in range(per_step):
-        b = f * per_step + t
+    outs = []
+    for b in range(half):
         l0, l1 = lt[b], lt[b + half]
         r0, r1 = rt[b], rt[b + half]
         lhs = jnp.concatenate([l0, l1], axis=0)
@@ -241,8 +236,13 @@
         both = lax.dot_general(
             lhs, rhs, (((0,), (0,)), ((), ())), preferred_element_type=jnp.float32
         )
-        out_ref[t, 0] = both[:, :cb].astype(out_ref.dtype)
-        out_ref[t, 1] = both[:, cb:].astype(out_ref.dtype)
+        out_v[b, 0] = both[:, :cb].astype(out_v.dtype)
+        out_v[b, 1] = both[:, cb:].astype(out_v.dtype)
+        cp = pltpu.make_async_copy(out_v.at[b], out_hbm.at[b], out_sems.at[b])
+        cp.start()
+        outs.append(cp)
+    for cp in outs:
+        cp.wait()
 
 
 def cross(left, right, scale):
@@ -250,19 +250,19 @@
     cb = right.shape[-1]
     bins = parts // 2
     chunks = 16
-    per_step = 8
     return pl.pallas_call(
         functools.partial(cross_kernel, scale, chunks),
         out_shape=jax.ShapeDtypeStruct((bins, 2, rb, cb), jnp.bfloat16),
-        grid=(bins // per_step,),
         in_specs=[pl.BlockSpec(memory_space=pl.ANY), pl.BlockSpec(memory_space=pl.ANY)],
-        out_specs=pl.BlockSpec((per_step, 2, rb, cb), lambda f: (f, 0, 0, 0)),
+        out_specs=pl.BlockSpec(memory_space=pl.ANY),
         scratch_shapes=[
             pltpu.VMEM((windows, parts, rb), left.dtype),
             pltpu.VMEM((windows, parts, cb), right.dtype),
             pltpu.VMEM((parts, windows, rb), left.dtype),
             pltpu.VMEM((parts, windows, cb), right.dtype),
+            pltpu.VMEM((bins, 2, rb, cb), jnp.bfloat16),
             pltpu.SemaphoreType.DMA((2, chunks)),
+            pltpu.SemaphoreType.DMA((bins,)),
         ],
         cost_estimate=pl.CostEstimate(
             flops=8 * bins * rb * cb * windows,

time: 66.2 us -> 65.2 us (0.985)
  Pallas kernels: 54.3 us -> 53.4 us
    pallas_call x1, Pallas kernels: 7.82 us -> 6.84 us  [cross(): pl.pallas_call(functools.partial(cross_kernel, scale, chunks), out_shape=...]
where the time goes in v19:
time: 65.2 us; the launch traced here: 65 us
  Pallas kernels  53.4 us (82%)
  matrix products  6.82 us (10%)
  local copies, waits for them, and re-layouts  2.06 us (3%)
  other arithmetic  2.02 us (3%)
  between operations  0.76 us (1%)
    pallas_call x1, Pallas kernels, exchange(): pl.pallas_call(functools.partial(exchange_kernel, nr, nc), out_shape=(jax...  46.5 us
    pallas_call x1, Pallas kernels, cross(): pl.pallas_call(functools.partial(cross_kernel, scale, chunks), out_shape=...  6.84 us
    dot_general x1, matrix products, on_device(): spectra = jnp.dot(placed, record, preferred_element_type=jnp.float32)[None]  6.36 us

profile of v19, /device:TPU:0, one launch (start us, length us, event | category | flops | bytes accessed | tf_op | source)
XLA Modules:
  0.0 65.0 jit_solution(11769141407625038915)
XLA Ops:
  0.7 0.7 %concatenate.7 = f32[257]{0:T(512)S(1)} pad(f32[101]{0:T(128)} %param.5, f32[]{:T(128)} %constant.31.clone.1), padding=0_156 | pad | bytes 1436 | tf_op jit(solution)/shard_map/concatenate | solution.py:40
  1.3 0.1 subtract_multiply_fusion
  1.4 1.1 %cosine_multiply_fusion = (f32[1,16,1280]{2,1,0:T(8,128)S(1)}, f32[1,16,1280]{2,1,0:T(8,128)S(1)}) fusion(f32[1280]{0:T(1024)S(1)} %subtract_multiply_fusion, s32[16]{0:T(128)} %param.6), kind=kLoop, calls=%fused_computation.26 | loop fusion | flops 245760 | bytes 169024 | tf_op jit(solution)/shard_map/mul | solution.py:26
  2.5 0.3 tile.10
  2.9 0.1 fusion.10
  3.1 0.5 fusion
  3.6 0.8 %dynamic_update_slice.3 = bf16[32,1408]{1,0:T(8,128)(2,1)S(1)} dynamic-update-slice(bf16[32,1408]{1,0:T(8,128)(2,1)S(1)} %broadcast_in_dim.2, bf16[32,1380]{1,0:T(8,128)(2,1)S(1)} %bitcast.35, s32[]{:T(128)} %constant.12.clone.1, s32[]{:T(128)S(6)} %select_n.22) | dynamic-update-slice | bytes 176644 | tf_op jit(solution)/shard_map/dynamic_update_slice | solution.py:190
  4.4 6.4 %fusion.18 = f32[32,4096]{1,0:T(8,128)S(1)} fusion(bf16[32,1408]{1,0:T(8,128)(2,1)S(1)} %dynamic_update_slice.3, bf16[1408,4096]{1,0:T(8,128)(2,1)} %param.4), kind=kOutput, calls=%fused_computation.33 | convolution fusion | flops 369098752 | bytes 12148736 | tf_op jit(solution)/shard_map/dot_general | solution.py:193
  10.8 0.1 fusion.9
  10.9 0.7 %fusion.1.w_ref = bf16[32,4096]{1,0:T(8,128)(2,1)} fusion(f32[32,4096]{1,0:T(8,128)S(1)} %fusion.18, f32[16,4096]{1,0:T(8,128)S(1)} %fusion.9), kind=kLoop, calls=%fused_computation.3 | loop fusion | flops 262144 | bytes 1048576 | tf_op jit(solution)/shard_map/convert_element_type | solution.py:60
  11.7 46.5 %shard_map.46 = (bf16[16,8,32,512]{3,2,1,0:T(8,128)(2,1)}, bf16[16,8,32,256]{3,2,1,0:T(8,128)(2,1)}) custom-call(bf16[32,4096]{1,0:T(8,128)(2,1)} %fusion.1.w_ref), custom_call_target="tpu_custom_call" | custom-call | tf_op jit(solution)/shard_map/pallas_call | solution.py:169
  58.2 6.8 %shard_map.47 = bf16[16,2,512,256]{3,2,1,0:T(8,128)(2,1)} custom-call(bf16[128,32,512]{2,1,0:T(8,128)(2,1)} %bitcast.32, bf16[128,32,256]{2,1,0:T(8,128)(2,1)} %bitcast.33), custom_call_target="tpu_custom_call" | custom-call | flops 2147483648 | bytes 14680064 | tf_op jit(solution)/shard_map/pallas_call | solution.py:253
  (7 shorter events, 0.1 us)

commit v20 on v19

--- a/solution.py
+++ b/solution.py
@@ -16,7 +16,7 @@
 floor_level = 0.5
 
 
-def analysis_kernel(fir_taps, bins):
+def analysis_kernel(fir_taps, bins, offset, length, slack):
     span = WL + TAPS - 1
     sample_times = jnp.arange(WL, dtype=jnp.int32)
     phase_index = bins[:, None] * sample_times[None, :] % WL
@@ -27,9 +27,10 @@
         2 * F, WL
     )
     lanes = 128
-    blocks = pl_cdiv(span, lanes)
+    assert slack + TAPS - 1 <= lanes
+    blocks = pl_cdiv(length, lanes)
     width = 2 * lanes
-    padded = jnp.pad(pattern, ((0, 0), (TAPS - 1, blocks * lanes + lanes - WL - (TAPS - 1))))
+    padded = jnp.pad(pattern, ((0, 0), (lanes, (blocks + 1) * lanes - WL - lanes)))
     windows = jnp.concatenate(
         [
             padded[:, : blocks * lanes].reshape(2 * F, blocks, lanes),
@@ -37,7 +38,9 @@
         ],
         axis=2,
     )
-    vector = jnp.concatenate([fir_taps, jnp.zeros((width + 1 - TAPS,), jnp.float32)])
+    vector = lax.dynamic_update_slice(
+        jnp.zeros((width + 1,), jnp.float32), fir_taps, (lanes - (TAPS - 1) - offset,)
+    )
     band = jnp.tile(vector, lanes)[: lanes * width].reshape(lanes, width)
     kernel = jnp.einsum(
         "bqs,rs->bqr",
@@ -45,7 +48,7 @@
         band,
         precision=lax.Precision.HIGHEST,
         preferred_element_type=jnp.float32,
-    ).reshape(2 * F, blocks * lanes)[:, :span]
+    ).reshape(2 * F, blocks * lanes)[:, :length]
     return kernel.astype(jnp.bfloat16)
 
 
@@ -182,14 +185,10 @@
 
 
 def on_device(record, fir_taps, bins, offsets):
-    kernel = analysis_kernel(fir_taps, bins)
-    span = WL + TAPS - 1
     local_count = offsets.shape[0]
-
     assert local_count == 1
-    placed = lax.dynamic_update_slice(
-        jnp.zeros((kernel.shape[0], record.shape[0]), kernel.dtype), kernel, (0, offsets[0])
-    )
+    slack = record.shape[0] - (WL + TAPS - 1)
+    placed = analysis_kernel(fir_taps, bins, offsets[0], record.shape[0], slack)
     spectra = jnp.dot(placed, record, preferred_element_type=jnp.float32)[None]
     whitened = whiten(spectra)
     channels = whitened.shape[-1]

time: 65.2 us -> 64.5 us (0.989)
  local copies, waits for them, and re-layouts: 2.06 us -> 1.31 us
    concatenate x1 -> x0, local copies, waits for them, and re-layouts: 0.66 us -> none  [analysis_kernel(): jnp.concatenate([fir_taps, jnp.zeros((width + 1 - TAPS,), jnp.float32)])]
where the time goes in v20:
time: 64.5 us; the launch traced here: 64.3 us
  Pallas kernels  53.4 us (83%)
  matrix products  6.85 us (11%)
  other arithmetic  2.02 us (3%)
  local copies, waits for them, and re-layouts  1.31 us (2%)
  between operations  0.75 us (1%)
    pallas_call x1, Pallas kernels, exchange(): pl.pallas_call(functools.partial(exchange_kernel, nr, nc), out_shape=(jax...  46.5 us
    pallas_call x1, Pallas kernels, cross(): pl.pallas_call(functools.partial(cross_kernel, scale, chunks), out_shape=...  6.84 us
    dot_general x1, matrix products, on_device(): spectra = jnp.dot(placed, record, preferred_element_type=jnp.float32)[None]  6.39 us

profile of v20, /device:TPU:0, one launch (start us, length us, event | category | flops | bytes accessed | tf_op | source)
XLA Modules:
  0.0 64.3 jit_solution(11491112427847938343)
XLA Ops:
  0.7 0.9 %dynamic_update_slice.5 = f32[257]{0:T(512)S(1)} dynamic-update-slice(f32[257]{0:T(512)S(1)} %tile.11, f32[101]{0:T(128)} %param.5, s32[]{:T(128)S(6)} %select_n.22) | dynamic-update-slice | bytes 812 | tf_op jit(solution)/shard_map/dynamic_update_slice | solution.py:41
  1.5 0.1 subtract_multiply_fusion
  1.6 1.1 %cosine_multiply_fusion = (f32[1,16,1280]{2,1,0:T(8,128)S(1)}, f32[1,16,1280]{2,1,0:T(8,128)S(1)}) fusion(f32[1280]{0:T(1024)S(1)} %subtract_multiply_fusion, s32[16]{0:T(128)} %param.6), kind=kLoop, calls=%fused_computation.28 | loop fusion | flops 245760 | bytes 169024 | tf_op jit(solution)/shard_map/mul | solution.py:26
  2.7 0.3 tile.13
  3.2 0.5 fusion
  3.6 6.4 %fusion.12 = f32[32,4096]{1,0:T(8,128)S(1)} fusion(bf16[1408,4096]{1,0:T(8,128)(2,1)} %param.4, bf16[11,4,8,128]{3,2,1,0:T(8,128)(2,1)S(1)} %fusion), kind=kOutput, calls=%fused_computation.22 | convolution fusion | flops 369098752 | bytes 12148736 | tf_op jit(solution)/shard_map/dot_general | solution.py:192
  10.0 0.1 fusion.9
  10.2 0.7 %fusion.1.w_ref = bf16[32,4096]{1,0:T(8,128)(2,1)} fusion(f32[32,4096]{1,0:T(8,128)S(1)} %fusion.12, f32[16,4096]{1,0:T(8,128)S(1)} %fusion.9), kind=kLoop, calls=%fused_computation.3 | loop fusion | flops 262144 | bytes 1048576 | tf_op jit(solution)/shard_map/convert_element_type | solution.py:63
  10.9 46.5 %shard_map.46 = (bf16[16,8,32,512]{3,2,1,0:T(8,128)(2,1)}, bf16[16,8,32,256]{3,2,1,0:T(8,128)(2,1)}) custom-call(bf16[32,4096]{1,0:T(8,128)(2,1)} %fusion.1.w_ref), custom_call_target="tpu_custom_call" | custom-call | tf_op jit(solution)/shard_map/pallas_call | solution.py:172
  57.5 6.8 %shard_map.47 = bf16[16,2,512,256]{3,2,1,0:T(8,128)(2,1)} custom-call(bf16[128,32,512]{2,1,0:T(8,128)(2,1)} %bitcast.28, bf16[128,32,256]{2,1,0:T(8,128)(2,1)} %bitcast.29), custom_call_target="tpu_custom_call" | custom-call | flops 2147483648 | bytes 14680064 | tf_op jit(solution)/shard_map/pallas_call | solution.py:252
  (7 shorter events, 0.1 us)

commit v21 on v20

--- a/solution.py
+++ b/solution.py
@@ -58,8 +58,8 @@
 
 def whiten(spectra):
     shaped = spectra.reshape(spectra.shape[0], 2, F, spectra.shape[-1])
-    magnitude = jnp.sqrt(shaped[:, 0] * shaped[:, 0] + shaped[:, 1] * shaped[:, 1])
-    inverse = 1.0 / jnp.maximum(magnitude, floor_level)
+    squared = shaped[:, 0] * shaped[:, 0] + shaped[:, 1] * shaped[:, 1]
+    inverse = jnp.minimum(lax.rsqrt(squared), 1.0 / floor_level)
     return (shaped * inverse[:, None]).astype(jnp.bfloat16)
 
 

time: 64.5 us -> 64.4 us (level)
  no operation moved by 1% of the time
where the time goes in v21:
time: 64.4 us; the launch traced here: 64.2 us
  Pallas kernels  53.4 us (83%)
  matrix products  6.85 us (11%)
  other arithmetic  1.96 us (3%)
  local copies, waits for them, and re-layouts  1.31 us (2%)
  between operations  0.75 us (1%)
    pallas_call x1, Pallas kernels, exchange(): pl.pallas_call(functools.partial(exchange_kernel, nr, nc), out_shape=(jax...  46.5 us
    pallas_call x1, Pallas kernels, cross(): pl.pallas_call(functools.partial(cross_kernel, scale, chunks), out_shape=...  6.84 us
    dot_general x1, matrix products, on_device(): spectra = jnp.dot(placed, record, preferred_element_type=jnp.float32)[None]  6.39 us

profile of v21, /device:TPU:0, one launch (start us, length us, event | category | flops | bytes accessed | tf_op | source)
XLA Modules:
  0.0 64.2 jit_solution(15754244562914513253)
XLA Ops:
  0.7 0.9 %dynamic_update_slice.5 = f32[257]{0:T(512)S(1)} dynamic-update-slice(f32[257]{0:T(512)S(1)} %tile.11, f32[101]{0:T(128)} %param.5, s32[]{:T(128)S(6)} %select_n.22) | dynamic-update-slice | bytes 812 | tf_op jit(solution)/shard_map/dynamic_update_slice | solution.py:41
  1.5 0.1 subtract_multiply_fusion
  1.6 1.1 %cosine_multiply_fusion = (f32[1,16,1280]{2,1,0:T(8,128)S(1)}, f32[1,16,1280]{2,1,0:T(8,128)S(1)}) fusion(f32[1280]{0:T(1024)S(1)} %subtract_multiply_fusion, s32[16]{0:T(128)} %param.6), kind=kLoop, calls=%fused_computation.27 | loop fusion | flops 245760 | bytes 169024 | tf_op jit(solution)/shard_map/mul | solution.py:26
  2.7 0.3 tile.13
  3.2 0.5 fusion
  3.6 6.4 %fusion.11 = f32[32,4096]{1,0:T(8,128)S(1)} fusion(bf16[1408,4096]{1,0:T(8,128)(2,1)} %param.4, bf16[11,4,8,128]{3,2,1,0:T(8,128)(2,1)S(1)} %fusion), kind=kOutput, calls=%fused_computation.21 | convolution fusion | flops 369098752 | bytes 12148736 | tf_op jit(solution)/shard_map/dot_general | solution.py:192
  10.0 0.1 fusion.8
  10.1 0.7 %fusion.1.w_ref = bf16[32,4096]{1,0:T(8,128)(2,1)} fusion(f32[32,4096]{1,0:T(8,128)S(1)} %fusion.11, f32[16,4096]{1,0:T(8,128)S(1)} %fusion.8), kind=kLoop, calls=%fused_computation.3 | loop fusion | flops 262144 | bytes 1048576 | tf_op jit(solution)/shard_map/convert_element_type | solution.py:63
  10.9 46.5 %shard_map.46 = (bf16[16,8,32,512]{3,2,1,0:T(8,128)(2,1)}, bf16[16,8,32,256]{3,2,1,0:T(8,128)(2,1)}) custom-call(bf16[32,4096]{1,0:T(8,128)(2,1)} %fusion.1.w_ref), custom_call_target="tpu_custom_call" | custom-call | tf_op jit(solution)/shard_map/pallas_call | solution.py:172
  57.4 6.8 %shard_map.47 = bf16[16,2,512,256]{3,2,1,0:T(8,128)(2,1)} custom-call(bf16[128,32,512]{2,1,0:T(8,128)(2,1)} %bitcast.28, bf16[128,32,256]{2,1,0:T(8,128)(2,1)} %bitcast.29), custom_call_target="tpu_custom_call" | custom-call | flops 2147483648 | bytes 14680064 | tf_op jit(solution)/shard_map/pallas_call | solution.py:252
  (7 shorter events, 0.1 us)

commit v22 on v20

--- a/solution.py
+++ b/solution.py
@@ -248,7 +248,7 @@
     windows, parts, rb = left.shape
     cb = right.shape[-1]
     bins = parts // 2
-    chunks = 16
+    chunks = 8
     return pl.pallas_call(
         functools.partial(cross_kernel, scale, chunks),
         out_shape=jax.ShapeDtypeStruct((bins, 2, rb, cb), jnp.bfloat16),

time: 64.5 us -> 64.3 us (level)
  no operation moved by 1% of the time
where the time goes in v22:
time: 64.3 us; the launch traced here: 64.2 us
  Pallas kernels  53.2 us (83%)
  matrix products  6.85 us (11%)
  other arithmetic  2.02 us (3%)
  local copies, waits for them, and re-layouts  1.31 us (2%)
  between operations  0.75 us (1%)
    pallas_call x1, Pallas kernels, exchange(): pl.pallas_call(functools.partial(exchange_kernel, nr, nc), out_shape=(jax...  46.5 us
    pallas_call x1, Pallas kernels, cross(): pl.pallas_call(functools.partial(cross_kernel, scale, chunks), out_shape=...  6.72 us
    dot_general x1, matrix products, on_device(): spectra = jnp.dot(placed, record, preferred_element_type=jnp.float32)[None]  6.39 us

profile of v22, /device:TPU:0, one launch (start us, length us, event | category | flops | bytes accessed | tf_op | source)
XLA Modules:
  0.0 64.2 jit_solution(16094637150320751278)
XLA Ops:
  0.7 0.9 %dynamic_update_slice.5 = f32[257]{0:T(512)S(1)} dynamic-update-slice(f32[257]{0:T(512)S(1)} %tile.11, f32[101]{0:T(128)} %param.5, s32[]{:T(128)S(6)} %select_n.22) | dynamic-update-slice | bytes 812 | tf_op jit(solution)/shard_map/dynamic_update_slice | solution.py:41
  1.5 0.1 subtract_multiply_fusion
  1.6 1.1 %cosine_multiply_fusion = (f32[1,16,1280]{2,1,0:T(8,128)S(1)}, f32[1,16,1280]{2,1,0:T(8,128)S(1)}) fusion(f32[1280]{0:T(1024)S(1)} %subtract_multiply_fusion, s32[16]{0:T(128)} %param.6), kind=kLoop, calls=%fused_computation.28 | loop fusion | flops 245760 | bytes 169024 | tf_op jit(solution)/shard_map/mul | solution.py:26
  2.7 0.3 tile.13
  3.2 0.5 fusion
  3.6 6.4 %fusion.12 = f32[32,4096]{1,0:T(8,128)S(1)} fusion(bf16[1408,4096]{1,0:T(8,128)(2,1)} %param.4, bf16[11,4,8,128]{3,2,1,0:T(8,128)(2,1)S(1)} %fusion), kind=kOutput, calls=%fused_computation.22 | convolution fusion | flops 369098752 | bytes 12148736 | tf_op jit(solution)/shard_map/dot_general | solution.py:192
  10.0 0.1 fusion.9
  10.2 0.7 %fusion.1.w_ref = bf16[32,4096]{1,0:T(8,128)(2,1)} fusion(f32[32,4096]{1,0:T(8,128)S(1)} %fusion.12, f32[16,4096]{1,0:T(8,128)S(1)} %fusion.9), kind=kLoop, calls=%fused_computation.3 | loop fusion | flops 262144 | bytes 1048576 | tf_op jit(solution)/shard_map/convert_element_type | solution.py:63
  10.9 46.5 %shard_map.46 = (bf16[16,8,32,512]{3,2,1,0:T(8,128)(2,1)}, bf16[16,8,32,256]{3,2,1,0:T(8,128)(2,1)}) custom-call(bf16[32,4096]{1,0:T(8,128)(2,1)} %fusion.1.w_ref), custom_call_target="tpu_custom_call" | custom-call | tf_op jit(solution)/shard_map/pallas_call | solution.py:172
  57.5 6.7 %shard_map.47 = bf16[16,2,512,256]{3,2,1,0:T(8,128)(2,1)} custom-call(bf16[128,32,512]{2,1,0:T(8,128)(2,1)} %bitcast.28, bf16[128,32,256]{2,1,0:T(8,128)(2,1)} %bitcast.29), custom_call_target="tpu_custom_call" | custom-call | flops 2147483648 | bytes 14680064 | tf_op jit(solution)/shard_map/pallas_call | solution.py:252
  (7 shorter events, 0.1 us)
